TPU v7x, 32 devices: a whole 2x2x4 slice. The times are simulated.
32 devices in a mesh: dp: 8 (over y, x, core), mp: 4 (over z).
Axes of the slice: x: 2, y: 2, z: 4, core: 2. Of those that a mesh axis runs over, the one named last changes fastest.
Arguments:
- tokens: bfloat16 [320, 4096], P('dp'), may hold values from -6 to 6
- attn_gain: float32 [4096], replicated, may hold values from 0.1 to 1.9
- head_gain: float32 [4096], replicated, may hold values from 0.1 to 1.9
- qkv_weight: bfloat16 [4096, 3, 4096], P('dp', None, 'mp'), may hold values from -0.09375 to 0.09375
- out_weight: bfloat16 [4096, 4096], P('mp', 'dp'), may hold values from -0.09375 to 0.09375
- head_weight: bfloat16 [4096, 1024], P('mp'), may hold values from -0.09375 to 0.09375
- key_cache: bfloat16 [320, 64, 4096], P('dp', None, 'mp'), may hold values from -400 to 400
- value_cache: bfloat16 [320, 64, 4096], P('dp', None, 'mp'), may hold values from -6 to 6
- parents: int32 [320], P('dp'), may hold values from 0 to 19
- allowed: int32 [320, 2], P('dp'), may hold values from 0 to 7, all different within a row
Outputs:
- new_stream: bfloat16 [320, 4096], P('dp')
- next_logits: float32 [320, 256], P('dp', 'mp')
Inputs may be any that keep to these rules, and one draw needn't show every extreme that they name: `parents`: a beam's parent is a beam of the same query. `allowed`: the 2 block ids of a beam differ.
All inputs are finite; a program needn't handle non-finite values.
Results may differ from a plain program's by a relative error of at most 0.017.
Values may be sent and summed in bfloat16 or wider, within the bound.
No kernel may reach another device: no remote copies, remote signals or barrier semaphores. Data moves between devices by JAX's collectives and lax.ppermute only.
A program may use at most 128 MiB of HBM per device.

v0:
```python
import jax
import jax.numpy as jnp
from jax import lax
from jax.sharding import PartitionSpec as P

HEAD = 128
BEAMS = 20
BLOCK = 128


def root_norm(values, gain_vec):
    float_values = values.astype(jnp.float32)
    factor = lax.rsqrt(jnp.mean(float_values * float_values, axis=-1, keepdims=True) + 1e-06)
    return float_values * factor * gain_vec


def select_blocks(whole_logits, allowed):
    block_count = whole_logits.shape[1] // BLOCK
    block_list = whole_logits.reshape(whole_logits.shape[0], block_count, BLOCK)
    one_hot_rows = (
        allowed[:, :, None] == jnp.arange(block_count, dtype=jnp.int32)[None, None, :]
    ).astype(jnp.float32)
    selected_token = jnp.einsum(
        "ioh,ihp->iop", one_hot_rows, block_list, precision=lax.Precision.HIGHEST
    )
    return selected_token.reshape(whole_logits.shape[0], -1)


def on_device(
    tokens,
    attn_gain,
    head_gain,
    qkv_weight,
    out_weight,
    head_weight,
    key_cache,
    value_cache,
    parents,
    allowed,
):
    row_count = tokens.shape[0]
    normed = root_norm(tokens, attn_gain).astype(jnp.bfloat16)
    spread = lax.all_to_all(normed, "dp", split_axis=1, concat_axis=0, tiled=True)
    depth_part = qkv_weight.shape[0]
    head_width = qkv_weight.shape[2]
    flat_qkv = qkv_weight.reshape(depth_part, 3 * head_width)
    projected = lax.psum_scatter(
        jnp.dot(spread, flat_qkv, preferred_element_type=jnp.float32),
        "dp",
        scatter_dimension=0,
        tiled=True,
    )
    projected = projected.astype(jnp.bfloat16).reshape(row_count, 3, head_width)
    local_heads = head_width // HEAD
    length = key_cache.shape[1] + 1
    source = jnp.arange(row_count, dtype=jnp.int32) // BEAMS * BEAMS + parents
    key_rows = jnp.concatenate(
        [jnp.take(key_cache, source, axis=0), projected[:, 1][:, None]], axis=1
    )
    value_rows = jnp.concatenate(
        [jnp.take(value_cache, source, axis=0), projected[:, 2][:, None]], axis=1
    )
    key_rows = key_rows.reshape(row_count, length, local_heads, HEAD)
    value_rows = value_rows.reshape(row_count, length, local_heads, HEAD)
    queries = projected[:, 0].reshape(row_count, local_heads, HEAD)
    scores = jnp.einsum(
        "thd,tjhd->thj", queries, key_rows, preferred_element_type=jnp.float32
    ) * HEAD ** (-0.5)
    softmax_w = jax.nn.softmax(scores, axis=-1).astype(jnp.bfloat16)
    attention_result = jnp.einsum(
        "thj,tjhd->thd", softmax_w, value_rows, preferred_element_type=jnp.float32
    )
    attention_result = attention_result.astype(jnp.bfloat16).reshape(row_count, head_width)
    partial_value = jnp.dot(
        attention_result,
        lax.all_gather(out_weight, "dp", axis=1, tiled=True),
        preferred_element_type=jnp.float32,
    )
    attn_out = lax.psum(partial_value, "mp")
    stream = tokens.astype(jnp.float32) + attn_out
    head_input = root_norm(stream, head_gain).astype(jnp.bfloat16)
    depth_rows = head_weight.shape[0]
    own_part = lax.dynamic_slice_in_dim(
        head_input, lax.axis_index("mp") * depth_rows, depth_rows, 1
    )
    partial_logits = jnp.dot(own_part, head_weight, preferred_element_type=jnp.float32)
    next_logits = lax.psum_scatter(
        select_blocks(partial_logits, allowed).astype(jnp.bfloat16),
        "mp",
        scatter_dimension=1,
        tiled=True,
    ).astype(jnp.float32)
    return (stream.astype(jnp.bfloat16), next_logits)


def solution(mesh):
    in_specs = (
        P("dp", None),
        P(),
        P(),
        P("dp", None, "mp"),
        P("mp", "dp"),
        P("mp", None),
        P("dp", None, "mp"),
        P("dp", None, "mp"),
        P("dp"),
        P("dp", None),
    )
    out_specs = (P("dp", None), P("dp", "mp"))
    return jax.shard_map(
        on_device, mesh=mesh, in_specs=in_specs, out_specs=out_specs, check_vma=False
    )
```

profile of v0, /device:TPU:0, one launch (start us, length us, event | category | flops | bytes accessed | tf_op | source)
XLA Modules:
  0.0 211.9 jit_solution(16103499963755374255)
XLA Ops:
  7.2 1.3 fusion.11
  8.5 1.1 fusion.13
  9.6 0.7 copy.55
  10.4 5.2 %all-to-all-start = ((bf16[40,8,512]{2,0,1:T(8,128)(2,1)}), bf16[40,8,512]{2,0,1:T(8,128)(2,1)S(1)}, u32[]{:S(2)}, u32[]{:S(2)}) async-start(bf16[40,8,512]{2,0,1:T(8,128)(2,1)} %bitcast.32), calls=%async_computation | async-start | bytes 655360 | tf_op jit(solution)/shard_map/all_to_all | solution.py:43
  15.6 4.7 %copy.24 = bf16[512,3,1024]{0,2,1:T(8,128)(2,1)} copy(bf16[512,3,1024]{2,0,1:T(8,128)(2,1)} %param.15) | data formatting | bytes 6291456 | tf_op args[3]
  20.3 2.9 %all-to-all-done = bf16[40,8,512]{2,0,1:T(8,128)(2,1)S(1)} async-done(((bf16[40,8,512]{2,0,1:T(8,128)(2,1)}), bf16[40,8,512]{2,0,1:T(8,128)(2,1)S(1)}, u32[]{:S(2)}, u32[]{:S(2)}) %all-to-all-start) | async-done | bytes 327712 | tf_op jit(solution)/shard_map/all_to_all | solution.py:43
  23.2 5.0 %fusion.35 = f32[320,3072]{1,0:T(8,128)} fusion(bf16[320,512]{1,0:T(8,128)(2,1)S(1)} %bitcast.34, bf16[512,3072]{0,1:T(8,128)(2,1)} %bitcast.33), kind=kOutput, calls=%fused_computation.57 | convolution fusion | flops 1006632960 | bytes 7405568 | tf_op jit(solution)/shard_map/dot_general | solution.py:48
  28.3 0.7 all-gather.2.cloned.1.call-update
  29.1 7.2 %gather_fusion = bf16[40,64,1024]{2,1,0:T(8,128)(2,1)} fusion(bf16[40,64,1024]{2,1,0:T(8,128)(2,1)} %param.18, s32[1024]{0:T(1024)S(1)} %pad_clamp_fusion), kind=kCustom, calls=%fused_computation.clone | custom fusion | bytes 10485920 | tf_op jit(solution)/shard_map/jit(_take)/gather | solution.py:58
  36.3 7.6 %gather_fusion.1 = bf16[40,64,1024]{2,1,0:T(8,128)(2,1)} fusion(bf16[40,64,1024]{2,1,0:T(8,128)(2,1)} %param.19, s32[1024]{0:T(1024)S(1)} %pad_clamp_fusion), kind=kCustom, calls=%fused_computation.1.clone | custom fusion | bytes 10485920 | tf_op jit(solution)/shard_map/jit(_take)/gather | solution.py:61
  43.8 9.1 %broadcast_select_fusion.1 = (bf16[40,64,1024]{2,1,0:T(8,128)(2,1)}, bf16[40,64,1024]{2,1,0:T(8,128)(2,1)}) fusion(bf16[40,64,1024]{2,1,0:T(8,128)(2,1)} %gather_fusion, pred[40]{0:T(512)(128)(4,1)S(1)} %get-tuple-element.5, bf16[40,64,1024]{2,1,0:T(8,128)(2,1)} %gather_fusion.1), kind=kLoop, calls=%fused_computation.11 | loop fusion | flops 5242880 | bytes 20971560 | tf_op jit(solution)/shard_map/jit(_take)/select_n | solution.py:58
  52.9 24.7 %reduce-scatter.5.cloned.1.call-done = f32[40,3072]{1,0:T(8,128)} async-done(((f32[320,3072]{1,0:T(8,128)}), f32[40,3072]{1,0:T(8,128)}) %reduce-scatter.5.cloned.1.call-update) | async-done | bytes 491536 | tf_op jit(solution)/shard_map/reduce_scatter | solution.py:47
  77.6 1.1 convert_element_type.34
  78.6 0.4 reshape.54
  79.0 0.3 fusion.32
  79.3 11.1 %pad_maximum_fusion = (bf16[40,65,1024]{2,1,0:T(8,128)(2,1)}, bf16[40,65,1024]{2,1,0:T(8,128)(2,1)}) fusion(bf16[40,1,1024]{2,1,0:T(2,128)(2,1)S(1)} %get-tuple-element.7, bf16[40,64,1024]{2,1,0:T(8,128)(2,1)} %get-tuple-element.9, bf16[40,1,1024]{2,1,0:T(2,128)(2,1)S(1)} %get-tuple-element.8, bf16[40,64,1024]{2,1,0:T(8,128)(2,1)} %get-tuple-element.10), kind=kLoop, calls=%fused_computation.4 | loop fusion | flops 21299200 | bytes 21299200 | tf_op jit(solution)/shard_map/concatenate | solution.py:57
  90.4 9.1 %reshape.86 = bf16[40,65,8,128]{3,2,1,0:T(8,128)(2,1)} reshape(bf16[40,65,1024]{2,1,0:T(8,128)(2,1)} %get-tuple-element.11) | data formatting | bytes 10649600 | tf_op jit(solution)/shard_map/reshape | solution.py:63
  99.5 9.3 %reshape.87 = bf16[40,65,8,128]{3,2,1,0:T(8,128)(2,1)} reshape(bf16[40,65,1024]{2,1,0:T(8,128)(2,1)} %get-tuple-element.12) | data formatting | bytes 10649600 | tf_op jit(solution)/shard_map/reshape | solution.py:64
  108.8 5.9 %fusion.4 = f32[40,8,1,65]{3,2,1,0:T(1,128)S(1)} fusion(bf16[40,65,8,128]{3,2,1,0:T(8,128)(2,1)} %reshape.86, bf16[40,3,1024]{2,1,0:T(4,128)(2,1)S(1)} %reshape.54), kind=kOutput, calls=%fused_computation.8 | convolution fusion | flops 5324800 | bytes 5571840 | tf_op jit(solution)/shard_map/thd,tjhd->thj/dot_general | solution.py:66
  114.9 4.2 %fusion.2 = f32[40,8,1,128]{3,2,1,0:T(1,128)S(1)} fusion(bf16[40,65,8,128]{3,2,1,0:T(8,128)(2,1)} %reshape.87, bf16[40,8,65,1]{2,1,0,3:T(8,128)(2,1)S(1)} %fusion.10), kind=kOutput, calls=%fused_computation.6 | convolution fusion | flops 5324800 | bytes 5530240 | tf_op jit(solution)/shard_map/thj,tjhd->thd/dot_general | solution.py:70
  119.1 16.2 %all-gather.2.cloned.1.call-done = bf16[1024,4096]{1,0:T(8,128)(2,1)} async-done(((bf16[1024,512]{1,0:T(8,128)(2,1)}), bf16[1024,4096]{1,0:T(8,128)(2,1)}) %all-gather.2.cloned.1.call-update) | async-done | bytes 8388624 | tf_op jit(solution)/shard_map/all_gather | solution.py:76
  135.3 5.9 %fusion.19 = f32[40,4096]{1,0:T(8,128)} fusion(bf16[1024,4096]{1,0:T(8,128)(2,1)} %all-gather.2.cloned.1.call-done, bf16[5,8,8,128]{3,2,1,0:T(8,128)(2,1)S(1)} %bitcast.36), kind=kOutput, calls=%fused_computation.34 | convolution fusion | flops 335544320 | bytes 9125888 | tf_op jit(solution)/shard_map/dot_general | solution.py:74
  141.4 0.7 dynamic-slice
  142.1 39.9 %all-reduce.2.cloned.1.call-done = f32[40,4096]{1,0:T(8,128)} async-done(((f32[40,4096]{1,0:T(8,128)}), f32[40,4096]{1,0:T(8,128)}) %all-reduce.2.cloned.1.call-update) | async-done | bytes 655376 | tf_op jit(solution)/shard_map/psum | solution.py:79
  181.9 1.3 multiply_reduce_fusion
  183.2 0.5 convolution_bitcast_fusion
  183.8 0.3 convolution_convert_fusion
  184.1 0.7 copy.40
  184.9 0.8 convert_element_type.37
  185.7 18.2 %reduce-scatter.7.cloned.1.call-done = bf16[64,40]{1,0:T(8,128)(2,1)} async-done(((bf16[256,40]{1,0:T(8,128)(2,1)}), bf16[64,40]{1,0:T(8,128)(2,1)}) %reduce-scatter.7.cloned.1.call-update) | async-done | bytes 5136
  203.9 0.8 copy.39
  204.7 0.6 convert_element_type.41
  (23 shorter events, 0.6 us)
Async XLA Ops:
  7.2 176.1 %copy-start = (bf16[1024,1024]{1,0:T(8,128)(2,1)S(1)}, bf16[1024,1024]{1,0:T(8,128)(2,1)}, u32[]{:S(2)}) copy-start(bf16[1024,1024]{1,0:T(8,128)(2,1)} %param.17) | copy-start | bytes 6291460
  10.4 12.8 %all-to-all-start = ((bf16[40,8,512]{2,0,1:T(8,128)(2,1)}), bf16[40,8,512]{2,0,1:T(8,128)(2,1)S(1)}, u32[]{:S(2)}, u32[]{:S(2)}) async-start(bf16[40,8,512]{2,0,1:T(8,128)(2,1)} %bitcast.32), calls=%async_computation | async-start | bytes 655360 | tf_op jit(solution)/shard_map/all_to_all | solution.py:43
  15.6 62.0 %reduce-scatter.5.cloned.1.call-start = ((), (), s32[]{:S(2)}) async-start(), calls=%async_computation.3 | async-start | bytes 4423680 | tf_op jit(solution)/shard_map/reduce_scatter | solution.py:47
  23.2 5.8 %copy-start.3 = (s32[40]{0:T(128)S(1)}, s32[40]{0:T(128)}, u32[]{:S(2)}) copy-start(s32[40]{0:T(128)} %param.20) | copy-start | bytes 484
  28.2 107.1 %all-gather.2.cloned.1.call-start = ((), (), s32[]{:S(2)}) async-start(), calls=%async_computation.4 | async-start | bytes 9437184 | tf_op jit(solution)/shard_map/all_gather | solution.py:76
  29.0 153.0 %all-reduce.2.cloned.1.call-start = ((), (), s32[]{:S(2)}) async-start(), calls=%async_computation.5 | async-start | bytes 1310720 | tf_op jit(solution)/shard_map/psum | solution.py:79
  135.3 6.0 %copy-start.2 = (s32[40,2]{0,1:T(2,128)S(1)}, s32[40,2]{0,1:T(2,128)}, u32[]{:S(2)}) copy-start(s32[40,2]{0,1:T(2,128)} %param.21) | copy-start | bytes 964
  135.3 46.6 %copy-start.1 = (bf16[40,4096]{1,0:T(8,128)(2,1)S(1)}, bf16[40,4096]{1,0:T(8,128)(2,1)}, u32[]{:S(2)}) copy-start(bf16[40,4096]{1,0:T(8,128)(2,1)} %param.12) | copy-start | bytes 983044
  141.2 62.7 %reduce-scatter.7.cloned.1.call-start = ((), (), s32[]{:S(2)}) async-start(), calls=%async_computation.6 | async-start | bytes 81920
Sparse Core Ops, SparseCore 0:
  28.3 49.1 reduce-scatter.4
  79.4 55.8 all-gather.1
  141.4 40.5 all-reduce.1
  185.0 18.8 reduce-scatter.6
where the time goes:
time: 213 us; the launch traced here: 212 us
  waiting for transfers between devices  103 us (48%)
  local copies, waits for them, and re-layouts  41.6 us (20%)
  other arithmetic  26.6 us (12%)
  matrix products  21.8 us (10%)
  between operations  13.9 us (7%)
  starting transfers between devices  5.36 us (3%)
    psum x1, waiting for transfers between devices, on_device(): attn_out = lax.psum(partial_value, 'mp')  39.9 us
    reduce_scatter x1, waiting for transfers between devices, on_device(): lax.psum_scatter(jnp.dot(spread, flat_qkv, preferred_element_type=jnp.flo...  24.7 us
    unnamed x5, waiting for transfers between devices  19 us
    all_gather x1, waiting for transfers between devices, on_device(): lax.all_gather(out_weight, 'dp', axis=1, tiled=True)  16.2 us
    concatenate x1, other arithmetic, on_device(): jnp.concatenate([jnp.take(key_cache, source, axis=0), projected[:, 1][:,...  11.1 us
    reshape x1, local copies, waits for them, and re-layouts, on_device(): value_rows = value_rows.reshape(row_count, length, local_heads, HEAD)  9.25 us
    reshape x1, local copies, waits for them, and re-layouts, on_device(): key_rows = key_rows.reshape(row_count, length, local_heads, HEAD)  9.11 us
    select_n x1, other arithmetic, on_device(): jnp.take(key_cache, source, axis=0)  9.08 us
  transfers between devices with their start and end apart: 5, of which 5 were waited for; matrix products, arithmetic and copies ran while one was open for 34% of the time, Pallas kernels for 0%

commit v1 on v0

v1 whole, which is shorter than its diff:
```python
import functools

import jax
import jax.numpy as jnp
from jax import lax
from jax.experimental import pallas as pl
from jax.experimental.pallas import tpu as pltpu
from jax.sharding import PartitionSpec as P

HEAD = 128
BEAMS = 20
BLOCK = 128
CORES = 2
LOW = -3e38
BF = jnp.bfloat16
F32 = jnp.float32

VM = pl.BlockSpec(memory_space=pltpu.VMEM)
SM = pl.BlockSpec(memory_space=pltpu.SMEM)


def shape(dims, kind):
    return jax.ShapeDtypeStruct(dims, kind)


def params(mib):
    return pltpu.CompilerParams(vmem_limit_bytes=mib * 2**20)


def cost(flops, moved):
    return pl.CostEstimate(flops=flops, bytes_accessed=moved, transcendentals=0)


def project_kernel(chips, place, *refs):
    pieces, (gain, own_w, other_w), outs, scratch = (
        refs[:chips],
        refs[chips : chips + 3],
        refs[chips + 3 : 2 * chips + 3],
        refs[-1],
    )
    rows = pieces[0].shape[0]
    depth = own_w.shape[1]

    @pl.when((pl.program_id(0) == 0) & (pl.program_id(1) == 0))
    def _():
        for k in range(chips):
            scratch[k * rows : (k + 1) * rows, :] = pieces[k][...].astype(F32) * gain[...]

    own_at = pl.multiple_of(place[0] * depth, depth)
    other_at = pl.multiple_of((1 - place[0]) * depth, depth)
    own_x = scratch[:, pl.ds(own_at, depth)].astype(BF)
    other_x = scratch[:, pl.ds(other_at, depth)].astype(BF)
    total = jnp.dot(own_x, own_w[0], preferred_element_type=F32) + jnp.dot(
        other_x, other_w[0], preferred_element_type=F32
    )
    for k in range(chips):
        outs[k][...] = total[k * rows : (k + 1) * rows].astype(outs[k].dtype)


def project(place, pieces, gain, own_w, other_w):
    chips = len(pieces)
    rows, width = pieces[0].shape
    _, depth, columns = own_w.shape
    tile = min(512, columns)
    steps = columns // tile
    whole = lambda dims: pl.BlockSpec(dims, lambda i, n: (0, 0))
    weight = pl.BlockSpec((1, depth, tile), lambda i, n: (i, 0, n))
    out = pl.BlockSpec((rows, tile), lambda i, n: (0, i * steps + n))
    return pl.pallas_call(
        functools.partial(project_kernel, chips),
        grid=(3, steps),
        in_specs=[SM] + [whole((rows, width))] * chips + [whole((1, width)), weight, weight],
        out_specs=[out] * chips,
        out_shape=[shape((rows, 3 * columns), BF if k else F32) for k in range(chips)],
        scratch_shapes=[pltpu.VMEM((chips * rows, width), F32)],
        compiler_params=params(24),
        cost_estimate=cost(2 * chips * rows * width * 3 * columns, 12 * depth * columns),
        name="project",
    )(place, *pieces, gain, own_w, other_w)


def attend_kernel(count, own, *refs):
    others = refs[: count - 1]
    factor, source, keys, values, out = refs[count - 1 :]
    rows, three = own.shape
    width = three // 3
    heads = width // HEAD
    cached = keys.shape[0] // rows
    total = own[...]
    for other in others:
        total += other[...].astype(F32)
    projected = (total * factor[...]).astype(BF)
    span = BEAMS * cached
    position = lax.broadcasted_iota(jnp.int32, (1, span), 1) // cached
    for group in range(rows // BEAMS):
        first = group * BEAMS
        low = first // 8 * 8
        high = -(-(first + BEAMS) // 8) * 8
        window = projected[low:high]
        parent = source[low:high] - first
        bias = jnp.where(position == parent, 0.0, LOW)
        token = lax.broadcasted_iota(jnp.int32, (high - low, 1), 0) + low
        mine = (token >= first) & (token < first + BEAMS)
        for head in range(heads):
            at = slice(head * HEAD, (head + 1) * HEAD)
            query = window[:, at]
            new_key = window[:, width + head * HEAD : width + (head + 1) * HEAD]
            new_value = window[:, 2 * width + head * HEAD : 2 * width + (head + 1) * HEAD]
            block = keys[first * cached : first * cached + span, at]
            score = (
                lax.dot_general(
                    query, block, (((1,), (1,)), ((), ())), preferred_element_type=F32
                )
                * HEAD ** (-0.5)
                + bias
            )
            new_score = jnp.sum(
                query.astype(F32) * new_key.astype(F32), axis=1, keepdims=True
            ) * HEAD ** (-0.5)
            top = jnp.maximum(jnp.max(score, axis=1, keepdims=True), new_score)
            weight = jnp.exp(score - top)
            new_weight = jnp.exp(new_score - top)
            scale = 1.0 / (jnp.sum(weight, axis=1, keepdims=True) + new_weight)
            weight = (weight * scale).astype(BF)
            new_weight = (new_weight * scale).astype(BF).astype(F32)
            result = (
                jnp.dot(
                    weight,
                    values[first * cached : first * cached + span, at],
                    preferred_element_type=F32,
                )
                + new_weight * new_value.astype(F32)
            )
            if low == first:
                out[low:high, at] = result.astype(out.dtype)
            else:
                out[low:high, at] = jnp.where(
                    mine, result, out[low:high, at].astype(F32)
                ).astype(out.dtype)


def attend(parts, factor, source, keys, values):
    rows, three = parts[0].shape
    width = three // 3
    span = keys.shape[0]
    return pl.pallas_call(
        functools.partial(attend_kernel, len(parts)),
        in_specs=[VM] * (len(parts) + 4),
        out_specs=VM,
        out_shape=shape((rows, width), BF),
        compiler_params=params(40),
        cost_estimate=cost(4 * rows * span * width, 4 * span * width),
        name="attend",
    )(*parts, factor, source, keys, values)


def output_kernel(chips, place, *refs):
    pieces, (own_w, other_w), outs = refs[:chips], refs[chips : chips + 2], refs[chips + 2 :]
    rows = pieces[0].shape[0]
    half = own_w.shape[1]
    joined = jnp.concatenate([piece[...].astype(F32) for piece in pieces], axis=0).astype(BF)
    for at, weight in ((place[0], own_w), (1 - place[0], other_w)):
        columns = pl.ds(pl.multiple_of(at * half, half), half)
        total = jnp.dot(joined, weight[...], preferred_element_type=F32)
        for k in range(chips):
            outs[k][:, columns] = total[k * rows : (k + 1) * rows].astype(BF)


def output(place, pieces, own_w, other_w):
    chips = len(pieces)
    rows = pieces[0].shape[0]
    width, half = own_w.shape
    return pl.pallas_call(
        functools.partial(output_kernel, chips),
        in_specs=[SM] + [VM] * (chips + 2),
        out_specs=[VM] * chips,
        out_shape=[shape((rows, CORES * half), BF)] * chips,
        compiler_params=params(16),
        cost_estimate=cost(4 * chips * rows * width * half, 4 * width * half),
        name="output",
    )(place, *pieces, own_w, other_w)


def logits_kernel(count, place, stream, gain, weight, allowed, *outs):
    value = stream[...]
    rows = value.shape[0]
    square = jnp.sum(value * value, axis=1, keepdims=True)
    whole = jnp.dot(
        (value * gain[...]).astype(BF), weight[...], preferred_element_type=F32
    )
    picked = []
    for slot in range(allowed.shape[1]):
        wanted = allowed[:, slot : slot + 1]
        total = jnp.zeros((rows, BLOCK), F32)
        for block in range(whole.shape[1] // BLOCK):
            total = jnp.where(
                wanted == block, whole[:, block * BLOCK : (block + 1) * BLOCK], total
            )
        picked.append(total)
    picked = jnp.concatenate(picked, axis=1)
    share = picked.shape[1] // count
    wide = outs[0].shape[1]
    lane = lax.broadcasted_iota(jnp.int32, (rows, wide), 1)
    tail = jnp.where(lane == share, square, 0.0)
    blocks = []
    for target in range(count):
        cut = picked[:, target * share : (target + 1) * share]
        blocks.append(jnp.concatenate([cut, tail[:, share:]], axis=1))
    for shift in range(count):
        target = lax.rem(place[1] + shift, count)
        total = blocks[0]
        for index in range(1, count):
            total = jnp.where(target == index, blocks[index], total)
        outs[shift][...] = total


def logits(place, stream, gain, weight, allowed, count):
    rows = stream.shape[0]
    share = allowed.shape[1] * BLOCK // count
    wide = (share + BLOCK) // BLOCK * BLOCK
    return pl.pallas_call(
        functools.partial(logits_kernel, count),
        in_specs=[SM] + [VM] * 4,
        out_specs=[VM] * count,
        out_shape=[shape((rows, wide), F32)] * count,
        compiler_params=params(16),
        cost_estimate=cost(2 * rows * weight.shape[0] * weight.shape[1], 2 * weight.size),
        name="logits",
    )(place, stream, gain, weight, allowed)


def finish_kernel(count, share, features, place, *refs):
    streams, sums, (stream_out, logits_out) = refs[:count], refs[count : 2 * count], refs[-2:]
    width = streams[0].shape[1]
    for shift in range(count):
        owner = lax.rem(place[1] + count - shift, count)
        columns = pl.ds(pl.multiple_of(owner * width, width), width)
        stream_out[:, columns] = streams[shift][...]
    total = sums[0][...]
    for shift in range(1, count):
        total += sums[shift][...]
    factor = lax.rsqrt(total[:, share : share + 1] * (1.0 / features) + 1e-06)
    logits_out[...] = total[:, :share] * factor


def finish(place, streams, sums, share):
    count = len(streams)
    rows, width = streams[0].shape
    return pl.pallas_call(
        functools.partial(finish_kernel, count, share, count * width),
        in_specs=[SM] + [VM] * (2 * count),
        out_specs=[VM, VM],
        out_shape=[shape((rows, count * width), BF), shape((rows, share), F32)],
        compiler_params=params(8),
        name="finish",
    )(place, *streams, *sums)


def on_device(
    dp,
    mp,
    tokens,
    attn_gain,
    head_gain,
    qkv_weight,
    out_weight,
    head_weight,
    key_cache,
    value_cache,
    parents,
    allowed,
):
    chips = dp // CORES
    rows, features = tokens.shape
    wide = features // chips
    here = lax.axis_index("dp")
    level = lax.axis_index("mp")
    chip, core = here // CORES, here % CORES
    place = jnp.stack([core, level]).astype(jnp.int32)

    def to_chip(value, k):
        return lax.ppermute(value, "dp", [(i, i ^ (CORES * k)) for i in range(dp)])

    def to_level(value, m):
        return lax.ppermute(value, "mp", [(i, (i + m) % mp) for i in range(mp)])

    def to_core(value):
        return lax.ppermute(value, "dp", [(i, i ^ 1) for i in range(dp)])

    def columns_of(value, index, width):
        return lax.dynamic_slice_in_dim(value, index * width, width, value.ndim - 1)

    blocks = [columns_of(tokens, chip ^ k, wide) for k in range(chips)]
    pieces = blocks[:1] + [to_chip(blocks[k], k) for k in range(1, chips)]
    own_qkv = jnp.transpose(qkv_weight, (1, 0, 2))
    other_qkv = to_core(own_qkv)
    other_out = to_core(out_weight)
    float_tokens = tokens.astype(F32)
    factor = lax.rsqrt(jnp.mean(float_tokens * float_tokens, axis=-1, keepdims=True) + 1e-06)
    gain = columns_of(attn_gain[None], chip, wide)

    parts = list(project(place, pieces, gain, own_qkv, other_qkv))
    parts = parts[:1] + [to_chip(parts[k], k) for k in range(1, chips)]

    source = jnp.arange(rows, dtype=jnp.int32) // BEAMS * BEAMS + parents
    head_width = key_cache.shape[2]
    attended = attend(
        parts,
        factor,
        source[:, None],
        key_cache.reshape(-1, head_width),
        value_cache.reshape(-1, head_width),
    )

    pieces = [attended] + [to_chip(attended, k) for k in range(1, chips)]
    parts = list(output(place, pieces, out_weight, other_out))
    parts = jnp.stack(parts[:1] + [to_chip(parts[k], k) for k in range(1, chips)])
    slices = [
        lax.dynamic_index_in_dim(parts, chip ^ ((level + m) % mp), 0, keepdims=False)
        for m in range(mp)
    ]
    total = slices[0].astype(F32)
    for m in range(1, mp):
        total += to_level(slices[m], m).astype(F32)
    stream = columns_of(tokens, level, wide).astype(F32) + total

    rounded = stream.astype(BF)
    streams = [rounded] + [to_level(rounded, m) for m in range(1, mp)]
    sums = logits(
        place, stream, columns_of(head_gain[None], level, wide), head_weight, allowed, mp
    )
    sums = list(sums[:1]) + [to_level(sums[m], m) for m in range(1, mp)]
    return tuple(finish(place, streams, sums, allowed.shape[1] * BLOCK // mp))


def solution(mesh):
    in_specs = (
        P("dp", None),
        P(),
        P(),
        P("dp", None, "mp"),
        P("mp", "dp"),
        P("mp", None),
        P("dp", None, "mp"),
        P("dp", None, "mp"),
        P("dp"),
        P("dp", None),
    )
    out_specs = (P("dp", None), P("dp", "mp"))
    return jax.shard_map(
        functools.partial(on_device, mesh.shape["dp"], mesh.shape["mp"]),
        mesh=mesh,
        in_specs=in_specs,
        out_specs=out_specs,
        check_vma=False,
    )
```

time: 213 us -> 91.1 us (0.43)
  waiting for transfers between devices: 103 us -> 31.2 us
  local copies, waits for them, and re-layouts: 41.6 us -> 12.1 us
  other arithmetic: 26.6 us -> 2.22 us
  starting transfers between devices: 5.36 us -> 28.4 us
  matrix products: 21.8 us -> 0 us
  Pallas kernels: 0 us -> 16.1 us
  between operations: 13.9 us -> 0.73 us
    psum x1 -> x0, waiting for transfers between devices: 39.9 us -> none  [on_device(): attn_out = lax.psum(partial_value, 'mp')]
    ppermute x0 -> x23, waiting for transfers between devices: none -> 31.2 us  [the longest x12 19.6 us: to_chip(): return lax.ppermute(value, 'dp', [(i, i ^ CORES * k) for i in range(dp)])]
    ppermute x0 -> x23, starting transfers between devices: none -> 28.4 us  [the longest x12 15 us: to_chip(): return lax.ppermute(value, 'dp', [(i, i ^ CORES * k) for i in range(dp)])]
    reduce_scatter x1 -> x0, waiting for transfers between devices: 24.7 us -> none  [on_device(): lax.psum_scatter(jnp.dot(spread, flat_qkv, preferred_element_type=jnp.flo...]
    dot_general x6 -> x0, matrix products: 21.8 us -> none  [the longest x1 5.88 us: on_device(): jnp.dot(attention_result, lax.all_gather(out_weight, 'dp', axis=1, tiled=...]
    unnamed x5 -> x0, waiting for transfers between devices: 19 us -> none
    reshape x3 -> x0, local copies, waits for them, and re-layouts: 18.7 us -> none  [the longest x1 9.25 us: on_device(): value_rows = value_rows.reshape(row_count, length, local_heads, HEAD)]
    all_gather x1 -> x0, waiting for transfers between devices: 16.2 us -> none  [on_device(): lax.all_gather(out_weight, 'dp', axis=1, tiled=True)]
  transfers between devices with their start and end apart: 5 -> 23, of which waited for: 5 -> 16; matrix products, arithmetic and copies ran while one was open for 34% -> 5% of each run, Pallas kernels for 0% -> 14%
where the time goes in v1:
time: 91.1 us; the launch traced here: 90.6 us
  waiting for transfers between devices  31.2 us (34%)
  starting transfers between devices  28.4 us (31%)
  Pallas kernels  16.1 us (18%)
  local copies, waits for them, and re-layouts  12.1 us (13%)
  other arithmetic  2.22 us (2%)
    ppermute x12, waiting for transfers between devices, to_chip(): return lax.ppermute(value, 'dp', [(i, i ^ CORES * k) for i in range(dp)])  19.6 us
    ppermute x12, starting transfers between devices, to_chip(): return lax.ppermute(value, 'dp', [(i, i ^ CORES * k) for i in range(dp)])  15 us
    ppermute x9, starting transfers between devices, to_level(): return lax.ppermute(value, 'mp', [(i, (i + m) % mp) for i in range(mp)])  12.7 us
    ppermute x9, waiting for transfers between devices, to_level(): return lax.ppermute(value, 'mp', [(i, (i + m) % mp) for i in range(mp)])  11.6 us
    unnamed x19, local copies, waits for them, and re-layouts  8.79 us
    pallas_call x1, Pallas kernels, attend(): pl.pallas_call(functools.partial(attend_kernel, len(parts)), in_specs=[VM...  7.68 us
    pallas_call x1, Pallas kernels, project(): pl.pallas_call(functools.partial(project_kernel, chips), grid=(3, steps),...  4.25 us
  transfers between devices with their start and end apart: 23, of which 16 were waited for; matrix products, arithmetic and copies ran while one was open for 5% of the time, Pallas kernels for 14%

profile of v1, /device:TPU:0, one launch (start us, length us, event | category | flops | bytes accessed | tf_op | source)
XLA Modules:
  0.0 90.6 jit_solution(813404334919356783)
XLA Ops:
  1.3 1.7 %constant_dynamic-slice_fusion = (bf16[40,1024]{1,0:T(8,128)(2,1)}, bf16[40,1024]{1,0:T(8,128)(2,1)}, bf16[40,1024]{1,0:T(8,128)(2,1)}, bf16[40,1024]{1,0:T(8,128)(2,1)S(1)}) fusion(bf16[40,4096]{1,0:T(8,128)(2,1)} %param.10, s32[]{:T(128)S(6)} %select_n.68, s32[]{:T(128)S(6)} %select_n.67, s32[]{:T(128)S(6)} %select_n.66, s32[]{:T(128)S(6)} %select_n.65), kind=kLoop, calls=%fused_computation.9 | loop fusion | bytes 655376 | tf_op jit(solution)/shard_map/dynamic_slice | solution.py:291
  3.0 2.9 %collective-permute-start = (bf16[40,1024]{1,0:T(8,128)(2,1)}, bf16[40,1024]{1,0:T(8,128)(2,1)S(1)}, u32[]{:S(2)}, u32[]{:S(2)}) collective-permute-start(bf16[40,1024]{1,0:T(8,128)(2,1)} %get-tuple-element.33), channel_id=1, source_target_pairs={{0,8},{4,12},{8,0},{12,4},{16,24},{20,28},{24,16},{28,20},{1,9},{5... | collective-permute-start | bytes 245768 | tf_op jit(solution)/shard_map/ppermute | solution.py:282
  5.9 1.5 %collective-permute-start.1 = (bf16[40,1024]{1,0:T(8,128)(2,1)}, bf16[40,1024]{1,0:T(8,128)(2,1)S(1)}, u32[]{:S(2)}, u32[]{:S(2)}) collective-permute-start(bf16[40,1024]{1,0:T(8,128)(2,1)} %get-tuple-element.32), channel_id=1, source_target_pairs={{0,16},{4,20},{8,24},{12,28},{16,0},{20,4},{24,8},{28,12},{1,17},{... | collective-permute-start | bytes 245768 | tf_op jit(solution)/shard_map/ppermute | solution.py:282
  8.1 1.1 %multiply_reduce_fusion = f32[40]{0:T(128)S(1)} fusion(bf16[40,4096]{1,0:T(8,128)(2,1)} %param.10), kind=kLoop, calls=%fused_computation | loop fusion | flops 491480 | bytes 327840 | tf_op jit(solution)/shard_map/reduce_sum | solution.py:299
  9.3 2.1 %collective-permute-done.1.refs_2_ = bf16[40,1024]{1,0:T(8,128)(2,1)S(1)} collective-permute-done((bf16[40,1024]{1,0:T(8,128)(2,1)}, bf16[40,1024]{1,0:T(8,128)(2,1)S(1)}, u32[]{:S(2)}, u32[]{:S(2)}) %collective-permute-start.1) | collective-permute-done | bytes 81952 | tf_op jit(solution)/shard_map/ppermute | solution.py:282
  11.4 1.5 %collective-permute-done.2.refs_3_ = bf16[40,1024]{1,0:T(8,128)(2,1)S(1)} collective-permute-done((bf16[40,1024]{1,0:T(8,128)(2,1)}, bf16[40,1024]{1,0:T(8,128)(2,1)S(1)}, u32[]{:S(2)}, u32[]{:S(2)}) %collective-permute-start.2) | collective-permute-done | bytes 81952 | tf_op jit(solution)/shard_map/ppermute | solution.py:282
  12.9 1.9 %copy-done.2 = bf16[512,3,1024]{2,0,1:T(8,128)(2,1)S(1)} copy-done((bf16[512,3,1024]{2,0,1:T(8,128)(2,1)S(1)}, bf16[512,3,1024]{2,0,1:T(8,128)(2,1)}, u32[]{:S(2)}) %copy-start.2) | copy-done | bytes 3145752
  14.8 4.3 %project.1 = (f32[40,3072]{1,0:T(8,128)S(1)}, bf16[40,3072]{1,0:T(8,128)(2,1)}, bf16[40,3072]{1,0:T(8,128)(2,1)}, bf16[40,3072]{1,0:T(8,128)(2,1)}) custom-call(s32[2]{0:T(128)S(1)} %pad_add_fusion.place, bf16[40,1024]{1,0:T(8,128)(2,1)S(1)} %get-tuple-element.34.refs_0_, bf16[40,1024]{1,0:T(8,128)(2,1)S(1)} %collective-permute-done.refs_1_, ...), custom_call_target="tpu_custom_call" | custom-call | flops 1006632960 | bytes 6291456 | tf_op jit(solution)/shard_map/project/pallas_call | solution.py:69
  21.1 2.2 %collective-permute-start.6 = (bf16[40,3072]{1,0:T(8,128)(2,1)}, bf16[40,3072]{1,0:T(8,128)(2,1)S(1)}, u32[]{:S(2)}, u32[]{:S(2)}) collective-permute-start(bf16[40,3072]{1,0:T(8,128)(2,1)} %get-tuple-element.17), channel_id=1, source_target_pairs={{0,24},{4,28},{8,16},{12,20},{16,8},{20,12},{24,0},{28,4},{1,25},{... | collective-permute-start | bytes 737288 | tf_op jit(solution)/shard_map/ppermute | solution.py:282
  23.6 5.3 %collective-permute-done.4.refs_0_ = bf16[40,3072]{1,0:T(8,128)(2,1)S(1)} collective-permute-done((bf16[40,3072]{1,0:T(8,128)(2,1)}, bf16[40,3072]{1,0:T(8,128)(2,1)S(1)}, u32[]{:S(2)}, u32[]{:S(2)}) %collective-permute-start.4) | collective-permute-done | bytes 245792 | tf_op jit(solution)/shard_map/ppermute | solution.py:282
  28.9 3.2 %collective-permute-done.5.refs_1_ = bf16[40,3072]{1,0:T(8,128)(2,1)S(1)} collective-permute-done((bf16[40,3072]{1,0:T(8,128)(2,1)}, bf16[40,3072]{1,0:T(8,128)(2,1)S(1)}, u32[]{:S(2)}, u32[]{:S(2)}) %collective-permute-start.5) | collective-permute-done | bytes 245792 | tf_op jit(solution)/shard_map/ppermute | solution.py:282
  32.2 2.5 %copy-done = bf16[40,64,1024]{2,1,0:T(8,128)(2,1)S(1)} copy-done((bf16[40,64,1024]{2,1,0:T(8,128)(2,1)S(1)}, bf16[40,64,1024]{2,1,0:T(8,128)(2,1)}, u32[]{:S(2)}) %copy-start) | copy-done | bytes 5242904
  34.7 2.5 %copy-done.1 = bf16[40,64,1024]{2,1,0:T(8,128)(2,1)S(1)} copy-done((bf16[40,64,1024]{2,1,0:T(8,128)(2,1)S(1)}, bf16[40,64,1024]{2,1,0:T(8,128)(2,1)}, u32[]{:S(2)}) %copy-start.1) | copy-done | bytes 5242904
  38.2 7.7 %attend.1.refs_0_ = bf16[40,1024]{1,0:T(8,128)(2,1)S(1)} custom-call(f32[40,3072]{1,0:T(8,128)S(1)} %copy-done.6, bf16[40,3072]{1,0:T(8,128)(2,1)S(1)} %collective-permute-done.4.refs_0_, bf16[40,3072]{1,0:T(8,128)(2,1)S(1)} %collective-permute-done.5.refs_1_, bf16[40,3072]{1,0:T(8,128)(2,1)S(1)} %collective-permute-done.6.refs_2_, ...), custom_call_target="tpu_custom_call" | custom-call | flops 419430400 | bytes 10485760 | tf_op jit(solution)/shard_map/attend/pallas_call | solution.py:146
  45.9 1.5 %collective-permute-start.7 = (bf16[40,1024]{1,0:T(8,128)(2,1)S(1)}, bf16[40,1024]{1,0:T(8,128)(2,1)S(1)}, u32[]{:S(2)}, u32[]{:S(2)}) collective-permute-start(bf16[40,1024]{1,0:T(8,128)(2,1)S(1)} %attend.1.refs_0_), channel_id=1, source_target_pairs={{0,8},{4,12},{8,0},{12,4},{16,24},{20,28},{24,16},{28,20},{1,9},{5... | collective-permute-start | bytes 245768 | tf_op jit(solution)/shard_map/ppermute | solution.py:282
  48.1 1.3 %collective-permute-start.9 = (bf16[40,1024]{1,0:T(8,128)(2,1)S(1)}, bf16[40,1024]{1,0:T(8,128)(2,1)S(1)}, u32[]{:S(2)}, u32[]{:S(2)}) collective-permute-start(bf16[40,1024]{1,0:T(8,128)(2,1)S(1)} %attend.1.refs_0_), channel_id=1, source_target_pairs={{0,24},{4,28},{8,16},{12,20},{16,8},{20,12},{24,0},{28,4},{1,25},{... | collective-permute-start | bytes 245768 | tf_op jit(solution)/shard_map/ppermute | solution.py:282
  50.4 1.4 %collective-permute-done.8.refs_2_ = bf16[40,1024]{1,0:T(8,128)(2,1)S(1)} collective-permute-done((bf16[40,1024]{1,0:T(8,128)(2,1)S(1)}, bf16[40,1024]{1,0:T(8,128)(2,1)S(1)}, u32[]{:S(2)}, u32[]{:S(2)}) %collective-permute-start.8) | collective-permute-done | bytes 81952 | tf_op jit(solution)/shard_map/ppermute | solution.py:282
  51.8 1.6 %collective-permute-done.9.refs_3_ = bf16[40,1024]{1,0:T(8,128)(2,1)S(1)} collective-permute-done((bf16[40,1024]{1,0:T(8,128)(2,1)S(1)}, bf16[40,1024]{1,0:T(8,128)(2,1)S(1)}, u32[]{:S(2)}, u32[]{:S(2)}) %collective-permute-start.9) | collective-permute-done | bytes 81952 | tf_op jit(solution)/shard_map/ppermute | solution.py:282
  53.5 1.7 %output.1 = (bf16[40,1024]{1,0:T(8,128)(2,1)S(1)}, bf16[40,1024]{1,0:T(8,128)(2,1)S(1)}, bf16[40,1024]{1,0:T(8,128)(2,1)S(1)}, bf16[40,1024]{1,0:T(8,128)(2,1)S(1)}) custom-call(s32[2]{0:T(128)S(1)} %pad_add_fusion.place, bf16[40,1024]{1,0:T(8,128)(2,1)S(1)} %attend.1.refs_0_, bf16[40,1024]{1,0:T(8,128)(2,1)S(1)} %collective-permute-done.7.refs_1_, ...), custom_call_target="tpu_custom_call" | custom-call | flops 335544320 | bytes 2097152 | tf_op jit(solution)/shard_map/output/pallas_call | solution.py:173
  55.2 1.3 %collective-permute-start.12 = (bf16[40,1024]{1,0:T(8,128)(2,1)S(1)}, bf16[40,1024]{1,0:T(8,128)(2,1)S(1)}, u32[]{:S(2)}, u32[]{:S(2)}) collective-permute-start(bf16[40,1024]{1,0:T(8,128)(2,1)S(1)} %get-tuple-element.20), channel_id=1, source_target_pairs={{0,16},{4,20},{8,24},{12,28},{16,0},{20,4},{24,8},{28,12},{1,17},{... | collective-permute-start | bytes 245768 | tf_op jit(solution)/shard_map/ppermute | solution.py:282
  57.6 1.1 %collective-permute-start.11 = (bf16[40,1024]{1,0:T(8,128)(2,1)S(1)}, bf16[40,1024]{1,0:T(8,128)(2,1)S(1)}, u32[]{:S(2)}, u32[]{:S(2)}) collective-permute-start(bf16[40,1024]{1,0:T(8,128)(2,1)S(1)} %get-tuple-element.19), channel_id=1, source_target_pairs={{0,8},{4,12},{8,0},{12,4},{16,24},{20,28},{24,16},{28,20},{1,9},{5... | collective-permute-start | bytes 245768 | tf_op jit(solution)/shard_map/ppermute | solution.py:282
  59.7 2.2 %collective-permute-done.13 = bf16[40,1024]{1,0:T(8,128)(2,1)S(1)} collective-permute-done((bf16[40,1024]{1,0:T(8,128)(2,1)S(1)}, bf16[40,1024]{1,0:T(8,128)(2,1)S(1)}, u32[]{:S(2)}, u32[]{:S(2)}) %collective-permute-start.13) | collective-permute-done | bytes 81952 | tf_op jit(solution)/shard_map/ppermute | solution.py:282
  62.2 1.6 %collective-permute-start.14 = (bf16[40,1024]{1,0:T(8,128)(2,1)S(1)}, bf16[40,1024]{1,0:T(8,128)(2,1)S(1)}, u32[]{:S(2)}, u32[]{:S(2)}) collective-permute-start(bf16[40,1024]{1,0:T(8,128)(2,1)S(1)} %get-tuple-element.28), channel_id=1, source_target_pairs={{0,1},{1,2},{2,3},{3,0},{4,5},{5,6},{6,7},{7,4},{8,9},{9,10},{10,1... | collective-permute-start | bytes 245768 | tf_op jit(solution)/shard_map/ppermute | solution.py:285
  63.8 2.6 %collective-permute-start.15 = (bf16[40,1024]{1,0:T(8,128)(2,1)S(1)}, bf16[40,1024]{1,0:T(8,128)(2,1)S(1)}, u32[]{:S(2)}, u32[]{:S(2)}) collective-permute-start(bf16[40,1024]{1,0:T(8,128)(2,1)S(1)} %get-tuple-element.30), channel_id=1, source_target_pairs={{0,2},{1,3},{2,0},{3,1},{4,6},{5,7},{6,4},{7,5},{8,10},{9,11},{10,... | collective-permute-start | bytes 245768 | tf_op jit(solution)/shard_map/ppermute | solution.py:285
  66.4 1.4 %collective-permute-start.16 = (bf16[40,1024]{1,0:T(8,128)(2,1)S(1)}, bf16[40,1024]{1,0:T(8,128)(2,1)S(1)}, u32[]{:S(2)}, u32[]{:S(2)}) collective-permute-start(bf16[40,1024]{1,0:T(8,128)(2,1)S(1)} %get-tuple-element.29), channel_id=1, source_target_pairs={{0,3},{1,0},{2,1},{3,2},{4,7},{5,4},{6,5},{7,6},{8,11},{9,8},{10,9... | collective-permute-start | bytes 245768 | tf_op jit(solution)/shard_map/ppermute | solution.py:285
  68.5 3.4 %collective-permute-done.15 = bf16[40,1024]{1,0:T(8,128)(2,1)S(1)} collective-permute-done((bf16[40,1024]{1,0:T(8,128)(2,1)S(1)}, bf16[40,1024]{1,0:T(8,128)(2,1)S(1)}, u32[]{:S(2)}, u32[]{:S(2)}) %collective-permute-start.15) | collective-permute-done | bytes 81952 | tf_op jit(solution)/shard_map/ppermute | solution.py:285
  73.6 2.0 %collective-permute-start.17 = (bf16[40,1024]{1,0:T(8,128)(2,1)S(1)}, bf16[40,1024]{1,0:T(8,128)(2,1)S(1)}, u32[]{:S(2)}, u32[]{:S(2)}) collective-permute-start(bf16[40,1024]{1,0:T(8,128)(2,1)S(1)} %get-tuple-element.26.refs_0_), channel_id=1, source_target_pairs={{0,1},{1,2},{2,3},{3,0},{4,5},{5,6},{6,7},{7,4},{8,9},{9,10},{10,1... | collective-permute-start | bytes 245768 | tf_op jit(solution)/shard_map/ppermute | solution.py:285
  75.6 1.5 %collective-permute-start.18 = (bf16[40,1024]{1,0:T(8,128)(2,1)S(1)}, bf16[40,1024]{1,0:T(8,128)(2,1)S(1)}, u32[]{:S(2)}, u32[]{:S(2)}) collective-permute-start(bf16[40,1024]{1,0:T(8,128)(2,1)S(1)} %get-tuple-element.26.refs_0_), channel_id=1, source_target_pairs={{0,2},{1,3},{2,0},{3,1},{4,6},{5,7},{6,4},{7,5},{8,10},{9,11},{10,... | collective-permute-start | bytes 245768 | tf_op jit(solution)/shard_map/ppermute | solution.py:285
  81.0 1.5 %collective-permute-start.21 = (f32[40,128]{1,0:T(8,128)S(1)}, f32[40,128]{1,0:T(8,128)S(1)}, u32[]{:S(2)}, u32[]{:S(2)}) collective-permute-start(f32[40,128]{1,0:T(8,128)S(1)} %get-tuple-element.24), channel_id=1, source_target_pairs={{0,2},{1,3},{2,0},{3,1},{4,6},{5,7},{6,4},{7,5},{8,10},{9,11},{10,... | collective-permute-start | bytes 61448 | tf_op jit(solution)/shard_map/ppermute | solution.py:285
  82.5 3.1 %collective-permute-done.20.refs_5_ = f32[40,128]{1,0:T(8,128)S(1)} collective-permute-done((f32[40,128]{1,0:T(8,128)S(1)}, f32[40,128]{1,0:T(8,128)S(1)}, u32[]{:S(2)}, u32[]{:S(2)}) %collective-permute-start.20) | collective-permute-done | bytes 20512 | tf_op jit(solution)/shard_map/ppermute | solution.py:285
  85.8 3.6 %collective-permute-done.22.refs_7_ = f32[40,128]{1,0:T(8,128)S(1)} collective-permute-done((f32[40,128]{1,0:T(8,128)S(1)}, f32[40,128]{1,0:T(8,128)S(1)}, u32[]{:S(2)}, u32[]{:S(2)}) %collective-permute-start.22) | collective-permute-done | bytes 20512 | tf_op jit(solution)/shard_map/ppermute | solution.py:285
  89.3 1.3 %finish.1 = (bf16[40,4096]{1,0:T(8,128)(2,1)}, f32[40,64]{1,0:T(8,128)}) custom-call(s32[2]{0:T(128)S(1)} %pad_add_fusion.place, bf16[40,1024]{1,0:T(8,128)(2,1)S(1)} %get-tuple-element.26.refs_0_, bf16[40,1024]{1,0:T(8,128)(2,1)S(1)} %collective-permute-done.17.refs_1_, bf16[40,1024]{1,0:T(8,128)(2,1)S(1)} %collective-permute-done.18.refs_2_, ...), custom_call_target="tpu_custom_call" | custom-call | tf_op jit(solution)/shard_map/finish/pallas_call | solution.py:249
  (50 shorter events, 15.3 us)
Async XLA Ops:
  0.6 12.3 %collective-permute-start.3 = (bf16[3,512,1024]{2,1,0:T(8,128)(2,1)}, bf16[3,512,1024]{2,1,0:T(8,128)(2,1)S(1)}, u32[]{:S(2)}, u32[]{:S(2)}) collective-permute-start(bf16[3,512,1024]{2,1,0:T(8,128)(2,1)} %bitcast.27), channel_id=1, source_target_pairs={{0,4},{4,0},{8,12},{12,8},{16,20},{20,16},{24,28},{28,24},{1,5},{5... | collective-permute-start | bytes 9437192 | tf_op jit(solution)/shard_map/ppermute | solution.py:288
  1.2 48.3 %collective-permute-start.10 = (bf16[1024,512]{1,0:T(8,128)(2,1)}, bf16[1024,512]{1,0:T(8,128)(2,1)}, u32[]{:S(2)}, u32[]{:S(2)}) collective-permute-start(bf16[1024,512]{1,0:T(8,128)(2,1)} %refs_4_.1), channel_id=1, source_target_pairs={{0,4},{4,0},{8,12},{12,8},{16,20},{20,16},{24,28},{28,24},{1,5},{5... | collective-permute-start | bytes 3145736 | tf_op jit(solution)/shard_map/ppermute | solution.py:288
  3.0 6.3 %collective-permute-start = (bf16[40,1024]{1,0:T(8,128)(2,1)}, bf16[40,1024]{1,0:T(8,128)(2,1)S(1)}, u32[]{:S(2)}, u32[]{:S(2)}) collective-permute-start(bf16[40,1024]{1,0:T(8,128)(2,1)} %get-tuple-element.33), channel_id=1, source_target_pairs={{0,8},{4,12},{8,0},{12,4},{16,24},{20,28},{24,16},{28,20},{1,9},{5... | collective-permute-start | bytes 245768 | tf_op jit(solution)/shard_map/ppermute | solution.py:282
  5.9 5.5 %collective-permute-start.1 = (bf16[40,1024]{1,0:T(8,128)(2,1)}, bf16[40,1024]{1,0:T(8,128)(2,1)S(1)}, u32[]{:S(2)}, u32[]{:S(2)}) collective-permute-start(bf16[40,1024]{1,0:T(8,128)(2,1)} %get-tuple-element.32), channel_id=1, source_target_pairs={{0,16},{4,20},{8,24},{12,28},{16,0},{20,4},{24,8},{28,12},{1,17},{... | collective-permute-start | bytes 245768 | tf_op jit(solution)/shard_map/ppermute | solution.py:282
  7.4 5.6 %collective-permute-start.2 = (bf16[40,1024]{1,0:T(8,128)(2,1)}, bf16[40,1024]{1,0:T(8,128)(2,1)S(1)}, u32[]{:S(2)}, u32[]{:S(2)}) collective-permute-start(bf16[40,1024]{1,0:T(8,128)(2,1)} %get-tuple-element.31), channel_id=1, source_target_pairs={{0,24},{4,28},{8,16},{12,20},{16,8},{20,12},{24,0},{28,4},{1,25},{... | collective-permute-start | bytes 245768 | tf_op jit(solution)/shard_map/ppermute | solution.py:282
  12.9 1.9 %copy-start.2 = (bf16[512,3,1024]{2,0,1:T(8,128)(2,1)S(1)}, bf16[512,3,1024]{2,0,1:T(8,128)(2,1)}, u32[]{:S(2)}) copy-start(bf16[512,3,1024]{2,0,1:T(8,128)(2,1)} %param.13) | copy-start | bytes 9437188
  14.8 8.6 %copy-start.8 = (s32[40]{0:T(128)S(1)}, s32[40]{0:T(128)}, u32[]{:S(2)}) copy-start(s32[40]{0:T(128)} %param.18) | copy-start | bytes 484
  19.1 0.8 copy-start.5
  19.9 9.0 %collective-permute-start.4 = (bf16[40,3072]{1,0:T(8,128)(2,1)}, bf16[40,3072]{1,0:T(8,128)(2,1)S(1)}, u32[]{:S(2)}, u32[]{:S(2)}) collective-permute-start(bf16[40,3072]{1,0:T(8,128)(2,1)} %get-tuple-element.15), channel_id=1, source_target_pairs={{0,8},{4,12},{8,0},{12,4},{16,24},{20,28},{24,16},{28,20},{1,9},{5... | collective-permute-start | bytes 737288 | tf_op jit(solution)/shard_map/ppermute | solution.py:282
  20.4 11.8 %collective-permute-start.5 = (bf16[40,3072]{1,0:T(8,128)(2,1)}, bf16[40,3072]{1,0:T(8,128)(2,1)S(1)}, u32[]{:S(2)}, u32[]{:S(2)}) collective-permute-start(bf16[40,3072]{1,0:T(8,128)(2,1)} %get-tuple-element.16), channel_id=1, source_target_pairs={{0,16},{4,20},{8,24},{12,28},{16,0},{20,4},{24,8},{28,12},{1,17},{... | collective-permute-start | bytes 737288 | tf_op jit(solution)/shard_map/ppermute | solution.py:282
  21.1 11.0 %collective-permute-start.6 = (bf16[40,3072]{1,0:T(8,128)(2,1)}, bf16[40,3072]{1,0:T(8,128)(2,1)S(1)}, u32[]{:S(2)}, u32[]{:S(2)}) collective-permute-start(bf16[40,3072]{1,0:T(8,128)(2,1)} %get-tuple-element.17), channel_id=1, source_target_pairs={{0,24},{4,28},{8,16},{12,20},{16,8},{20,12},{24,0},{28,4},{1,25},{... | collective-permute-start | bytes 737288 | tf_op jit(solution)/shard_map/ppermute | solution.py:282
  32.2 2.5 %copy-start = (bf16[40,64,1024]{2,1,0:T(8,128)(2,1)S(1)}, bf16[40,64,1024]{2,1,0:T(8,128)(2,1)}, u32[]{:S(2)}) copy-start(bf16[40,64,1024]{2,1,0:T(8,128)(2,1)} %param.16) | copy-start | bytes 15728644
  34.7 2.5 %copy-start.1 = (bf16[40,64,1024]{2,1,0:T(8,128)(2,1)S(1)}, bf16[40,64,1024]{2,1,0:T(8,128)(2,1)}, u32[]{:S(2)}) copy-start(bf16[40,64,1024]{2,1,0:T(8,128)(2,1)} %param.17) | copy-start | bytes 15728644
  37.1 1.0 %copy-start.6 = (f32[40,3072]{1,0:T(8,128)S(1)}, f32[40,3072]{1,0:T(8,128)}, u32[]{:S(2)}) copy-start(f32[40,3072]{1,0:T(8,128)} %copy-done.5) | copy-start | bytes 1474564
  38.2 15.3 %copy-start.4 = (bf16[1024,512]{1,0:T(8,128)(2,1)S(1)}, bf16[1024,512]{1,0:T(8,128)(2,1)}, u32[]{:S(2)}) copy-start(bf16[1024,512]{1,0:T(8,128)(2,1)} %refs_4_.1) | copy-start | bytes 3145732
  45.9 32.9 %copy-start.7 = (s32[40,2]{0,1:T(2,128)S(1)}, s32[40,2]{0,1:T(2,128)}, u32[]{:S(2)}) copy-start(s32[40,2]{0,1:T(2,128)} %param.19) | copy-start | bytes 964
  45.9 32.9 %copy-start.3 = (bf16[1024,1024]{1,0:T(8,128)(2,1)S(1)}, bf16[1024,1024]{1,0:T(8,128)(2,1)}, u32[]{:S(2)}) copy-start(bf16[1024,1024]{1,0:T(8,128)(2,1)} %weight.1) | copy-start | bytes 6291460
  45.9 4.5 %collective-permute-start.7 = (bf16[40,1024]{1,0:T(8,128)(2,1)S(1)}, bf16[40,1024]{1,0:T(8,128)(2,1)S(1)}, u32[]{:S(2)}, u32[]{:S(2)}) collective-permute-start(bf16[40,1024]{1,0:T(8,128)(2,1)S(1)} %attend.1.refs_0_), channel_id=1, source_target_pairs={{0,8},{4,12},{8,0},{12,4},{16,24},{20,28},{24,16},{28,20},{1,9},{5... | collective-permute-start | bytes 245768 | tf_op jit(solution)/shard_map/ppermute | solution.py:282
  47.4 4.4 %collective-permute-start.8 = (bf16[40,1024]{1,0:T(8,128)(2,1)S(1)}, bf16[40,1024]{1,0:T(8,128)(2,1)S(1)}, u32[]{:S(2)}, u32[]{:S(2)}) collective-permute-start(bf16[40,1024]{1,0:T(8,128)(2,1)S(1)} %attend.1.refs_0_), channel_id=1, source_target_pairs={{0,16},{4,20},{8,24},{12,28},{16,0},{20,4},{24,8},{28,12},{1,17},{... | collective-permute-start | bytes 245768 | tf_op jit(solution)/shard_map/ppermute | solution.py:282
  48.1 5.3 %collective-permute-start.9 = (bf16[40,1024]{1,0:T(8,128)(2,1)S(1)}, bf16[40,1024]{1,0:T(8,128)(2,1)S(1)}, u32[]{:S(2)}, u32[]{:S(2)}) collective-permute-start(bf16[40,1024]{1,0:T(8,128)(2,1)S(1)} %attend.1.refs_0_), channel_id=1, source_target_pairs={{0,24},{4,28},{8,16},{12,20},{16,8},{20,12},{24,0},{28,4},{1,25},{... | collective-permute-start | bytes 245768 | tf_op jit(solution)/shard_map/ppermute | solution.py:282
  55.2 4.5 %collective-permute-start.12 = (bf16[40,1024]{1,0:T(8,128)(2,1)S(1)}, bf16[40,1024]{1,0:T(8,128)(2,1)S(1)}, u32[]{:S(2)}, u32[]{:S(2)}) collective-permute-start(bf16[40,1024]{1,0:T(8,128)(2,1)S(1)} %get-tuple-element.20), channel_id=1, source_target_pairs={{0,16},{4,20},{8,24},{12,28},{16,0},{20,4},{24,8},{28,12},{1,17},{... | collective-permute-start | bytes 245768 | tf_op jit(solution)/shard_map/ppermute | solution.py:282
  56.6 5.3 %collective-permute-start.13 = (bf16[40,1024]{1,0:T(8,128)(2,1)S(1)}, bf16[40,1024]{1,0:T(8,128)(2,1)S(1)}, u32[]{:S(2)}, u32[]{:S(2)}) collective-permute-start(bf16[40,1024]{1,0:T(8,128)(2,1)S(1)} %get-tuple-element.21), channel_id=1, source_target_pairs={{0,24},{4,28},{8,16},{12,20},{16,8},{20,12},{24,0},{28,4},{1,25},{... | collective-permute-start | bytes 245768 | tf_op jit(solution)/shard_map/ppermute | solution.py:282
  57.6 4.4 %collective-permute-start.11 = (bf16[40,1024]{1,0:T(8,128)(2,1)S(1)}, bf16[40,1024]{1,0:T(8,128)(2,1)S(1)}, u32[]{:S(2)}, u32[]{:S(2)}) collective-permute-start(bf16[40,1024]{1,0:T(8,128)(2,1)S(1)} %get-tuple-element.19), channel_id=1, source_target_pairs={{0,8},{4,12},{8,0},{12,4},{16,24},{20,28},{24,16},{28,20},{1,9},{5... | collective-permute-start | bytes 245768 | tf_op jit(solution)/shard_map/ppermute | solution.py:282
  62.2 6.3 %collective-permute-start.14 = (bf16[40,1024]{1,0:T(8,128)(2,1)S(1)}, bf16[40,1024]{1,0:T(8,128)(2,1)S(1)}, u32[]{:S(2)}, u32[]{:S(2)}) collective-permute-start(bf16[40,1024]{1,0:T(8,128)(2,1)S(1)} %get-tuple-element.28), channel_id=1, source_target_pairs={{0,1},{1,2},{2,3},{3,0},{4,5},{5,6},{6,7},{7,4},{8,9},{9,10},{10,1... | collective-permute-start | bytes 245768 | tf_op jit(solution)/shard_map/ppermute | solution.py:285
  63.8 8.1 %collective-permute-start.15 = (bf16[40,1024]{1,0:T(8,128)(2,1)S(1)}, bf16[40,1024]{1,0:T(8,128)(2,1)S(1)}, u32[]{:S(2)}, u32[]{:S(2)}) collective-permute-start(bf16[40,1024]{1,0:T(8,128)(2,1)S(1)} %get-tuple-element.30), channel_id=1, source_target_pairs={{0,2},{1,3},{2,0},{3,1},{4,6},{5,7},{6,4},{7,5},{8,10},{9,11},{10,... | collective-permute-start | bytes 245768 | tf_op jit(solution)/shard_map/ppermute | solution.py:285
  66.4 6.3 %collective-permute-start.16 = (bf16[40,1024]{1,0:T(8,128)(2,1)S(1)}, bf16[40,1024]{1,0:T(8,128)(2,1)S(1)}, u32[]{:S(2)}, u32[]{:S(2)}) collective-permute-start(bf16[40,1024]{1,0:T(8,128)(2,1)S(1)} %get-tuple-element.29), channel_id=1, source_target_pairs={{0,3},{1,0},{2,1},{3,2},{4,7},{5,4},{6,5},{7,6},{8,11},{9,8},{10,9... | collective-permute-start | bytes 245768 | tf_op jit(solution)/shard_map/ppermute | solution.py:285
  73.6 15.8 %collective-permute-start.17 = (bf16[40,1024]{1,0:T(8,128)(2,1)S(1)}, bf16[40,1024]{1,0:T(8,128)(2,1)S(1)}, u32[]{:S(2)}, u32[]{:S(2)}) collective-permute-start(bf16[40,1024]{1,0:T(8,128)(2,1)S(1)} %get-tuple-element.26.refs_0_), channel_id=1, source_target_pairs={{0,1},{1,2},{2,3},{3,0},{4,5},{5,6},{6,7},{7,4},{8,9},{9,10},{10,1... | collective-permute-start | bytes 245768 | tf_op jit(solution)/shard_map/ppermute | solution.py:285
  75.6 13.7 %collective-permute-start.18 = (bf16[40,1024]{1,0:T(8,128)(2,1)S(1)}, bf16[40,1024]{1,0:T(8,128)(2,1)S(1)}, u32[]{:S(2)}, u32[]{:S(2)}) collective-permute-start(bf16[40,1024]{1,0:T(8,128)(2,1)S(1)} %get-tuple-element.26.refs_0_), channel_id=1, source_target_pairs={{0,2},{1,3},{2,0},{3,1},{4,6},{5,7},{6,4},{7,5},{8,10},{9,11},{10,... | collective-permute-start | bytes 245768 | tf_op jit(solution)/shard_map/ppermute | solution.py:285
  77.1 12.3 %collective-permute-start.19 = (bf16[40,1024]{1,0:T(8,128)(2,1)S(1)}, bf16[40,1024]{1,0:T(8,128)(2,1)S(1)}, u32[]{:S(2)}, u32[]{:S(2)}) collective-permute-start(bf16[40,1024]{1,0:T(8,128)(2,1)S(1)} %get-tuple-element.26.refs_0_), channel_id=1, source_target_pairs={{0,3},{1,0},{2,1},{3,2},{4,7},{5,4},{6,5},{7,6},{8,11},{9,8},{10,9... | collective-permute-start | bytes 245768 | tf_op jit(solution)/shard_map/ppermute | solution.py:285
  79.9 5.6 %collective-permute-start.20 = (f32[40,128]{1,0:T(8,128)S(1)}, f32[40,128]{1,0:T(8,128)S(1)}, u32[]{:S(2)}, u32[]{:S(2)}) collective-permute-start(f32[40,128]{1,0:T(8,128)S(1)} %get-tuple-element.23), channel_id=1, source_target_pairs={{0,1},{1,2},{2,3},{3,0},{4,5},{5,6},{6,7},{7,4},{8,9},{9,10},{10,1... | collective-permute-start | bytes 61448 | tf_op jit(solution)/shard_map/ppermute | solution.py:285
  81.0 4.7 %collective-permute-start.21 = (f32[40,128]{1,0:T(8,128)S(1)}, f32[40,128]{1,0:T(8,128)S(1)}, u32[]{:S(2)}, u32[]{:S(2)}) collective-permute-start(f32[40,128]{1,0:T(8,128)S(1)} %get-tuple-element.24), channel_id=1, source_target_pairs={{0,2},{1,3},{2,0},{3,1},{4,6},{5,7},{6,4},{7,5},{8,10},{9,11},{10,... | collective-permute-start | bytes 61448 | tf_op jit(solution)/shard_map/ppermute | solution.py:285
  85.5 3.8 %collective-permute-start.22 = (f32[40,128]{1,0:T(8,128)S(1)}, f32[40,128]{1,0:T(8,128)S(1)}, u32[]{:S(2)}, u32[]{:S(2)}) collective-permute-start(f32[40,128]{1,0:T(8,128)S(1)} %get-tuple-element.25), channel_id=1, source_target_pairs={{0,3},{1,0},{2,1},{3,2},{4,7},{5,4},{6,5},{7,6},{8,11},{9,8},{10,9... | collective-permute-start | bytes 61448 | tf_op jit(solution)/shard_map/ppermute | solution.py:285

commit v2 on v1

v2 whole, which is shorter than its diff:
```python
import functools

import jax
import jax.numpy as jnp
from jax import lax
from jax.experimental import pallas as pl
from jax.experimental.pallas import tpu as pltpu
from jax.sharding import PartitionSpec as P

HEAD = 128
BEAMS = 20
BLOCK = 128
CORES = 2
LOW = -3e38
BF = jnp.bfloat16
F32 = jnp.float32

VM = pl.BlockSpec(memory_space=pltpu.VMEM)
SM = pl.BlockSpec(memory_space=pltpu.SMEM)
ANY = pl.BlockSpec(memory_space=pl.ANY)


def shape(dims, kind):
    return jax.ShapeDtypeStruct(dims, kind)


def params(mib):
    return pltpu.CompilerParams(vmem_limit_bytes=mib * 2**20)


def cost(flops, moved):
    return pl.CostEstimate(flops=flops, bytes_accessed=moved, transcendentals=0)


def split_kernel(chips, place, tokens, *refs):
    outs, sems = refs[: chips + 1], refs[chips + 1]
    width = outs[0].shape[1]
    copies = []
    for k in range(chips + 1):
        index = place[2] ^ k if k < chips else place[1]
        columns = pl.ds(pl.multiple_of(index * width, width), width)
        copies.append(pltpu.make_async_copy(tokens.at[:, columns], outs[k], sems.at[k]))
    for copy in copies[1:] + copies[:1]:
        copy.start()
    for copy in copies:
        copy.wait()


def split(place, tokens, chips):
    rows, features = tokens.shape
    return pl.pallas_call(
        functools.partial(split_kernel, chips),
        in_specs=[SM, ANY],
        out_specs=[VM] * (chips + 1),
        out_shape=[shape((rows, features // chips), tokens.dtype)] * (chips + 1),
        scratch_shapes=[pltpu.SemaphoreType.DMA((chips + 1,))],
        compiler_params=params(4),
        cost_estimate=cost(0, 4 * tokens.size),
        name="split",
    )(place, tokens)


def fetch_kernel(count, *refs):
    sources, targets, sems = refs[:count], refs[count : 2 * count], refs[2 * count]
    copies = []
    for i in range(count):
        pieces = 4 if sources[i].shape[0] % 32 == 0 else 1
        size = sources[i].shape[0] // pieces
        for n in range(pieces):
            part = pl.ds(n * size, size)
            copies.append(
                pltpu.make_async_copy(
                    sources[i].at[part], targets[i].at[part], sems.at[4 * i + n]
                )
            )
    for copy in copies:
        copy.start()
    for copy in copies:
        copy.wait()


def fetch(name, *sources):
    count = len(sources)
    return pl.pallas_call(
        functools.partial(fetch_kernel, count),
        in_specs=[ANY] * count,
        out_specs=[VM] * count,
        out_shape=[shape(source.shape, source.dtype) for source in sources],
        scratch_shapes=[pltpu.SemaphoreType.DMA((4 * count,))],
        compiler_params=params(16),
        cost_estimate=cost(0, sum(4 * source.size for source in sources)),
        name=name,
    )(*sources)


def project_kernel(chips, place, *refs):
    pieces, (gain, own_w, other_w) = refs[:chips], refs[chips : chips + 3]
    outs, scratch = refs[chips + 3 : 2 * chips + 3], refs[-1]
    rows, width = pieces[0].shape
    depth = own_w.shape[0] // 3
    columns = own_w.shape[1]
    scaled = gain[:, pl.ds(pl.multiple_of(place[2] * width, width), width)]
    for k in range(chips):
        scratch[k * rows : (k + 1) * rows, :] = pieces[k][...].astype(F32) * scaled
    own_at = pl.multiple_of(place[0] * depth, depth)
    other_at = pl.multiple_of((1 - place[0]) * depth, depth)
    own_x = scratch[:, pl.ds(own_at, depth)].astype(BF)
    other_x = scratch[:, pl.ds(other_at, depth)].astype(BF)
    tile = min(512, columns)
    for i in range(3):
        for n in range(columns // tile):
            at = slice(n * tile, (n + 1) * tile)
            total = jnp.dot(
                own_x, own_w[i * depth : (i + 1) * depth, at], preferred_element_type=F32
            ) + jnp.dot(
                other_x, other_w[i * depth : (i + 1) * depth, at], preferred_element_type=F32
            )
            to = slice(i * columns + n * tile, i * columns + (n + 1) * tile)
            for k in range(chips):
                outs[k][:, to] = total[k * rows : (k + 1) * rows].astype(BF)


def project(place, pieces, gain, own_w, other_w):
    chips = len(pieces)
    rows, width = pieces[0].shape
    columns = own_w.shape[1]
    return pl.pallas_call(
        functools.partial(project_kernel, chips),
        in_specs=[SM] + [VM] * (chips + 3),
        out_specs=[VM] * chips,
        out_shape=[shape((rows, 3 * columns), BF)] * chips,
        scratch_shapes=[pltpu.VMEM((chips * rows, width), F32)],
        compiler_params=params(12),
        cost_estimate=cost(2 * chips * rows * width * 3 * columns, 4 * own_w.size),
        name="project",
    )(place, *pieces, gain, own_w, other_w)


def attend_kernel(count, *refs):
    parts = refs[:count]
    tokens, source, keys, values, out, scores, sums = refs[count:]
    rows, three = parts[0].shape
    width = three // 3
    heads = width // HEAD
    cached = keys.shape[0] // rows
    total = parts[0][...].astype(F32)
    for part in parts[1:]:
        total += part[...].astype(F32)
    stream = tokens[...].astype(F32)
    factor = lax.rsqrt(jnp.mean(stream * stream, axis=1, keepdims=True) + 1e-06)
    projected = (total * factor).astype(BF)
    span = BEAMS * cached
    groups = rows // BEAMS
    position = lax.broadcasted_iota(jnp.int32, (1, span), 1) // cached
    windows = []
    for group in range(groups):
        first = group * BEAMS
        windows.append((first // 8 * 8, -(-(first + BEAMS) // 8) * 8))
    size = max(high - low for low, high in windows)
    for group, (low, high) in enumerate(windows):
        for head in range(heads):
            at = slice(head * HEAD, (head + 1) * HEAD)
            block = keys[group * span : (group + 1) * span, at]
            place = (group * heads + head) * size
            scores[place : place + high - low, :] = lax.dot_general(
                projected[low:high, at],
                block,
                (((1,), (1,)), ((), ())),
                preferred_element_type=F32,
            )
    unit = HEAD ** (-0.5) * 1.4426950408889634
    news = []
    for group, (low, high) in enumerate(windows):
        first = group * BEAMS
        bias = jnp.where(position == source[low:high] - first, 0.0, LOW)
        for head in range(heads):
            at = slice(head * HEAD, (head + 1) * HEAD)
            key_at = slice(width + head * HEAD, width + (head + 1) * HEAD)
            place = (group * heads + head) * size
            score = scores[place : place + high - low, :] * unit + bias
            new_score = (
                jnp.sum(
                    projected[low:high, at].astype(F32) * projected[low:high, key_at].astype(F32),
                    axis=1,
                    keepdims=True,
                )
                * unit
            )
            top = jnp.maximum(jnp.max(score, axis=1, keepdims=True), new_score)
            weight = jnp.exp2(score - top)
            new_weight = jnp.exp2(new_score - top)
            scale = 1.0 / (jnp.sum(weight, axis=1, keepdims=True) + new_weight)
            sums[place : place + high - low, :] = weight.astype(BF).astype(F32)
            news.append((new_weight, scale))
    for group, (low, high) in enumerate(windows):
        first = group * BEAMS
        token = lax.broadcasted_iota(jnp.int32, (high - low, 1), 0) + low
        mine = (token >= first) & (token < first + BEAMS)
        for head in range(heads):
            at = slice(head * HEAD, (head + 1) * HEAD)
            value_at = slice(2 * width + head * HEAD, 2 * width + (head + 1) * HEAD)
            place = (group * heads + head) * size
            new_weight, scale = news[group * heads + head]
            result = (
                jnp.dot(
                    sums[place : place + high - low, :].astype(BF),
                    values[group * span : (group + 1) * span, at],
                    preferred_element_type=F32,
                )
                + new_weight.astype(BF).astype(F32) * projected[low:high, value_at].astype(F32)
            ) * scale
            if low == first:
                out[low:high, at] = result.astype(out.dtype)
            else:
                out[low:high, at] = jnp.where(
                    mine, result, out[low:high, at].astype(F32)
                ).astype(out.dtype)


def attend(parts, tokens, source, keys, values):
    rows, three = parts[0].shape
    width = three // 3
    cached = keys.shape[0] // rows
    stack = rows // BEAMS * (width // HEAD) * (-(-BEAMS // 8) * 8 + 8)
    return pl.pallas_call(
        functools.partial(attend_kernel, len(parts)),
        in_specs=[VM] * (len(parts) + 4),
        out_specs=VM,
        out_shape=shape((rows, width), BF),
        scratch_shapes=[pltpu.VMEM((stack, BEAMS * cached), F32)] * 2,
        compiler_params=params(14),
        cost_estimate=cost(4 * rows * BEAMS * cached * width, 4 * keys.size),
        name="attend",
    )(*parts, tokens, source, keys, values)


def output_kernel(chips, place, *refs):
    pieces, (own_w, other_w), outs = refs[:chips], refs[chips : chips + 2], refs[chips + 2 :]
    rows = pieces[0].shape[0]
    half = own_w.shape[1]
    joined = jnp.concatenate([piece[...].astype(F32) for piece in pieces], axis=0).astype(BF)
    for at, weight in ((place[0], own_w), (1 - place[0], other_w)):
        columns = pl.ds(pl.multiple_of(at * half, half), half)
        total = jnp.dot(joined, weight[...], preferred_element_type=F32)
        for k in range(chips):
            outs[k][:, columns] = total[k * rows : (k + 1) * rows].astype(BF)


def output(place, pieces, own_w, other_w):
    chips = len(pieces)
    rows = pieces[0].shape[0]
    width, half = own_w.shape
    return pl.pallas_call(
        functools.partial(output_kernel, chips),
        in_specs=[SM] + [VM] * (chips + 2),
        out_specs=[VM] * chips,
        out_shape=[shape((rows, CORES * half), BF)] * chips,
        compiler_params=params(16),
        cost_estimate=cost(4 * chips * rows * width * half, 4 * width * half),
        name="output",
    )(place, *pieces, own_w, other_w)


def logits_kernel(count, place, *refs):
    partials, (tokens, gain, weight, allowed) = refs[:count], refs[count : count + 4]
    own_stream, own_tail, outs = refs[count + 4], refs[count + 5], refs[count + 6 :]
    rows, width = tokens.shape
    value = partials[0][...].astype(F32)
    for partial in partials[1:]:
        value += partial[...].astype(F32)
    value += tokens[...].astype(F32)
    rounded = value.astype(BF)
    own_stream[...] = rounded
    for out in outs:
        out[:, :width] = rounded
    square = jnp.sum(value * value, axis=1, keepdims=True)
    scaled = gain[:, pl.ds(pl.multiple_of(place[1] * width, width), width)]
    whole = jnp.dot((value * scaled).astype(BF), weight[...], preferred_element_type=F32)
    picked = []
    for slot in range(allowed.shape[1]):
        wanted = allowed[:, slot : slot + 1]
        total = jnp.zeros((rows, BLOCK), F32)
        for block in range(whole.shape[1] // BLOCK):
            total = jnp.where(
                wanted == block, whole[:, block * BLOCK : (block + 1) * BLOCK], total
            )
        picked.append(total)
    picked = jnp.concatenate(picked, axis=1)
    share = picked.shape[1] // count
    wide = own_tail.shape[1]
    lane = lax.broadcasted_iota(jnp.int32, (rows, wide), 1)
    coarse = square.astype(BF).astype(F32)
    tail = jnp.where(lane == share, coarse, jnp.where(lane == share + 1, square - coarse, 0.0))
    blocks = []
    for target in range(count):
        cut = picked[:, target * share : (target + 1) * share]
        blocks.append(jnp.concatenate([cut, tail[:, share:]], axis=1))
    for shift in range(count):
        target = lax.rem(place[1] + shift, count)
        total = blocks[0]
        for index in range(1, count):
            total = jnp.where(target == index, blocks[index], total)
        if shift == 0:
            own_tail[...] = total
        else:
            outs[shift - 1][:, width:] = total.astype(BF)


def logits(place, partials, tokens, gain, weight, allowed):
    count = len(partials)
    rows, width = tokens.shape
    share = allowed.shape[1] * BLOCK // count
    wide = (share + 1 + BLOCK) // BLOCK * BLOCK
    return pl.pallas_call(
        functools.partial(logits_kernel, count),
        in_specs=[SM] + [VM] * (count + 4),
        out_specs=[VM] * (count + 1),
        out_shape=[shape((rows, width), BF), shape((rows, wide), F32)]
        + [shape((rows, width + wide), BF)] * (count - 1),
        compiler_params=params(8),
        cost_estimate=cost(2 * rows * weight.shape[0] * weight.shape[1], 2 * weight.size),
        name="logits",
    )(place, *partials, tokens, gain, weight, allowed)


def finish_kernel(count, share, place, own_stream, own_tail, *refs):
    others, (stream_out, logits_out) = refs[: count - 1], refs[-2:]
    width = own_stream.shape[1]

    def columns(shift):
        owner = lax.rem(place[1] + count - shift, count)
        return pl.ds(pl.multiple_of(owner * width, width), width)

    stream_out[:, columns(0)] = own_stream[...]
    total = own_tail[...]
    for shift in range(1, count):
        stream_out[:, columns(shift)] = others[shift - 1][:, :width]
        total += others[shift - 1][:, width:].astype(F32)
    square = total[:, share : share + 1] + total[:, share + 1 : share + 2]
    factor = lax.rsqrt(square * (1.0 / (count * width)) + 1e-06)
    logits_out[...] = total[:, :share] * factor


def finish(place, own_stream, own_tail, others, share):
    count = len(others) + 1
    rows, width = own_stream.shape
    return pl.pallas_call(
        functools.partial(finish_kernel, count, share),
        in_specs=[SM] + [VM] * (count + 1),
        out_specs=[VM, VM],
        out_shape=[shape((rows, count * width), BF), shape((rows, share), F32)],
        compiler_params=params(4),
        name="finish",
    )(place, own_stream, own_tail, *others)


def on_device(
    dp,
    mp,
    tokens,
    attn_gain,
    head_gain,
    qkv_weight,
    out_weight,
    head_weight,
    key_cache,
    value_cache,
    parents,
    allowed,
):
    chips = dp // CORES
    rows = tokens.shape[0]
    here = lax.axis_index("dp")
    level = lax.axis_index("mp")
    chip, core = here // CORES, here % CORES
    place = jnp.stack([core, level, chip]).astype(jnp.int32)

    def to_chip(value, k):
        return lax.ppermute(value, "dp", [(i, i ^ (CORES * k)) for i in range(dp)])

    def to_level(value, m):
        return lax.ppermute(value, "mp", [(i, (i + m) % mp) for i in range(mp)])

    def to_core(value):
        return lax.ppermute(value, "dp", [(i, i ^ 1) for i in range(dp)])

    *blocks, level_tokens = split(place, tokens, chips)
    pieces = blocks[:1] + [to_chip(blocks[k], k) for k in range(1, chips)]
    own_qkv = jnp.transpose(qkv_weight, (1, 0, 2)).reshape(-1, qkv_weight.shape[2])
    other_qkv = to_core(own_qkv)
    other_out = to_core(out_weight)
    own_qkv, _ = lax.optimization_barrier((own_qkv, blocks[0]))
    (own_qkv,) = fetch("fetch_qkv", own_qkv)

    parts = list(project(place, pieces, attn_gain[None], own_qkv, other_qkv))
    head_width = key_cache.shape[2]
    caches = (key_cache.reshape(-1, head_width), value_cache.reshape(-1, head_width))
    caches, _ = lax.optimization_barrier((caches, parts[0]))
    keys, values = fetch("fetch_cache", *caches)
    parts = parts[:1] + [to_chip(parts[k], k) for k in range(1, chips)]

    source = jnp.arange(rows, dtype=jnp.int32) // BEAMS * BEAMS + parents
    attended = attend(parts, tokens, source[:, None], keys, values)

    pieces = [attended] + [to_chip(attended, k) for k in range(1, chips)]
    parts = list(output(place, pieces, out_weight, other_out))
    parts = jnp.stack(parts[:1] + [to_chip(parts[k], k) for k in range(1, chips)])
    slices = [
        lax.dynamic_index_in_dim(parts, chip ^ ((level + m) % mp), 0, keepdims=False)
        for m in range(mp)
    ]
    slices = slices[:1] + [to_level(slices[m], m) for m in range(1, mp)]
    own_stream, own_tail, *others = logits(
        place, slices, level_tokens, head_gain[None], head_weight, allowed
    )
    others = [to_level(other, m + 1) for m, other in enumerate(others)]
    return tuple(finish(place, own_stream, own_tail, others, allowed.shape[1] * BLOCK // mp))


def solution(mesh):
    in_specs = (
        P("dp", None),
        P(),
        P(),
        P("dp", None, "mp"),
        P("mp", "dp"),
        P("mp", None),
        P("dp", None, "mp"),
        P("dp", None, "mp"),
        P("dp"),
        P("dp", None),
    )
    out_specs = (P("dp", None), P("dp", "mp"))
    return jax.shard_map(
        functools.partial(on_device, mesh.shape["dp"], mesh.shape["mp"]),
        mesh=mesh,
        in_specs=in_specs,
        out_specs=out_specs,
        check_vma=False,
    )
```

time: 91.1 us -> 70.2 us (0.77)
  waiting for transfers between devices: 31.2 us -> 22.9 us
  local copies, waits for them, and re-layouts: 12.1 us -> 8.08 us
  Pallas kernels: 16.1 us -> 12.3 us
  starting transfers between devices: 28.4 us -> 25.8 us
  other arithmetic: 2.22 us -> 0.13 us
    ppermute x12, waiting for transfers between devices: 19.6 us -> 13.4 us  [to_chip(): return lax.ppermute(value, 'dp', [(i, i ^ CORES * k) for i in range(dp)])]
    pallas_call x1, Pallas kernels: 7.68 us -> 3.67 us  [attend(): pl.pallas_call(functools.partial(attend_kernel, len(parts)), in_specs=[VM...]
    ppermute x9 -> x6, starting transfers between devices: 12.7 us -> 10 us  [to_level(): return lax.ppermute(value, 'mp', [(i, (i + m) % mp) for i in range(mp)])]
    ppermute x9 -> x6, waiting for transfers between devices: 11.6 us -> 9.53 us  [to_level(): return lax.ppermute(value, 'mp', [(i, (i + m) % mp) for i in range(mp)])]
    dynamic_slice x1 -> x0, local copies, waits for them, and re-layouts: 1.7 us -> none  [columns_of(): return lax.dynamic_slice_in_dim(value, index * width, width, value.ndim - 1)]
    another operation x2 -> x0, local copies, waits for them, and re-layouts: 1.38 us -> none
    reduce_sum x1 -> x0, other arithmetic: 1.14 us -> none  [on_device(): jnp.mean(float_tokens * float_tokens, axis=-1, keepdims=True) + 1e-06]
    convert_element_type x1 -> x0, other arithmetic: 0.95 us -> none  [on_device(): rounded = stream.astype(BF)]
  transfers between devices with their start and end apart: 23 -> 20, of which waited for: 16 -> 15; matrix products, arithmetic and copies ran while one was open for 5% -> 0% of each run, Pallas kernels for 14% -> 12%
where the time goes in v2:
time: 70.2 us; the launch traced here: 69.9 us
  starting transfers between devices  25.8 us (37%)
  waiting for transfers between devices  22.9 us (33%)
  Pallas kernels  12.3 us (18%)
  local copies, waits for them, and re-layouts  8.08 us (12%)
  between operations  0.76 us (1%)
    ppermute x12, starting transfers between devices, to_chip(): return lax.ppermute(value, 'dp', [(i, i ^ CORES * k) for i in range(dp)])  15.1 us
    ppermute x12, waiting for transfers between devices, to_chip(): return lax.ppermute(value, 'dp', [(i, i ^ CORES * k) for i in range(dp)])  13.4 us
    ppermute x6, starting transfers between devices, to_level(): return lax.ppermute(value, 'mp', [(i, (i + m) % mp) for i in range(mp)])  10 us
    ppermute x6, waiting for transfers between devices, to_level(): return lax.ppermute(value, 'mp', [(i, (i + m) % mp) for i in range(mp)])  9.53 us
    unnamed x23, local copies, waits for them, and re-layouts  7.96 us
    pallas_call x1, Pallas kernels, attend(): pl.pallas_call(functools.partial(attend_kernel, len(parts)), in_specs=[VM...  3.67 us
    pallas_call x1, Pallas kernels, project(): pl.pallas_call(functools.partial(project_kernel, chips), in_specs=[SM] +...  2.64 us
    pallas_call x1, Pallas kernels, output(): pl.pallas_call(functools.partial(output_kernel, chips), in_specs=[SM] + [...  1.74 us
  transfers between devices with their start and end apart: 20, of which 15 were waited for; matrix products, arithmetic and copies ran while one was open for 0% of the time, Pallas kernels for 12%

profile of v2, /device:TPU:0, one launch (start us, length us, event | category | flops | bytes accessed | tf_op | source)
XLA Modules:
  0.0 69.9 jit_solution(1313203260025096625)
XLA Ops:
  1.4 1.0 %copy-done.4 = bf16[40,4096]{1,0:T(8,128)(2,1)S(1)} copy-done((bf16[40,4096]{1,0:T(8,128)(2,1)S(1)}, bf16[40,4096]{1,0:T(8,128)(2,1)}, u32[]{:S(2)}) %copy-start.4) | copy-done | bytes 327704
  3.0 3.0 %collective-permute-start = (bf16[40,1024]{1,0:T(8,128)(2,1)S(1)}, bf16[40,1024]{1,0:T(8,128)(2,1)S(1)}, u32[]{:S(2)}, u32[]{:S(2)}) collective-permute-start(bf16[40,1024]{1,0:T(8,128)(2,1)S(1)} %get-tuple-element.26), channel_id=1, source_target_pairs={{0,8},{4,12},{8,0},{12,4},{16,24},{20,28},{24,16},{28,20},{1,9},{5... | collective-permute-start | bytes 245768 | tf_op jit(solution)/shard_map/ppermute | solution.py:379
  6.0 1.5 %collective-permute-start.1 = (bf16[40,1024]{1,0:T(8,128)(2,1)S(1)}, bf16[40,1024]{1,0:T(8,128)(2,1)S(1)}, u32[]{:S(2)}, u32[]{:S(2)}) collective-permute-start(bf16[40,1024]{1,0:T(8,128)(2,1)S(1)} %get-tuple-element.27), channel_id=1, source_target_pairs={{0,16},{4,20},{8,24},{12,28},{16,0},{20,4},{24,8},{28,12},{1,17},{... | collective-permute-start | bytes 245768 | tf_op jit(solution)/shard_map/ppermute | solution.py:379
  7.6 1.9 %copy-done.2 = bf16[512,3,1024]{2,0,1:T(8,128)(2,1)S(1)} copy-done((bf16[512,3,1024]{2,0,1:T(8,128)(2,1)S(1)}, bf16[512,3,1024]{2,0,1:T(8,128)(2,1)}, u32[]{:S(2)}) %copy-start.2) | copy-done | bytes 3145752
  9.7 1.5 %collective-permute-done.1.refs_2_ = bf16[40,1024]{1,0:T(8,128)(2,1)S(1)} collective-permute-done((bf16[40,1024]{1,0:T(8,128)(2,1)S(1)}, bf16[40,1024]{1,0:T(8,128)(2,1)S(1)}, u32[]{:S(2)}, u32[]{:S(2)}) %collective-permute-start.1) | collective-permute-done | bytes 81952 | tf_op jit(solution)/shard_map/ppermute | solution.py:379
  11.2 1.6 %collective-permute-done.2.refs_3_ = bf16[40,1024]{1,0:T(8,128)(2,1)S(1)} collective-permute-done((bf16[40,1024]{1,0:T(8,128)(2,1)S(1)}, bf16[40,1024]{1,0:T(8,128)(2,1)S(1)}, u32[]{:S(2)}, u32[]{:S(2)}) %collective-permute-start.2) | collective-permute-done | bytes 81952 | tf_op jit(solution)/shard_map/ppermute | solution.py:379
  12.9 2.6 %project.1 = (bf16[40,3072]{1,0:T(8,128)(2,1)S(1)}, bf16[40,3072]{1,0:T(8,128)(2,1)}, bf16[40,3072]{1,0:T(8,128)(2,1)}, bf16[40,3072]{1,0:T(8,128)(2,1)}) custom-call(s32[3]{0:T(128)S(1)} %pad_add_fusion.place, bf16[40,1024]{1,0:T(8,128)(2,1)S(1)} %get-tuple-element.25.refs_0_, bf16[40,1024]{1,0:T(8,128)(2,1)S(1)} %collective-permute-done.refs_1_, ...), custom_call_target="tpu_custom_call" | custom-call | flops 1006632960 | bytes 6291456 | tf_op jit(solution)/shard_map/project/pallas_call | solution.py:127
  16.8 2.2 %collective-permute-start.6 = (bf16[40,3072]{1,0:T(8,128)(2,1)}, bf16[40,3072]{1,0:T(8,128)(2,1)S(1)}, u32[]{:S(2)}, u32[]{:S(2)}) collective-permute-start(bf16[40,3072]{1,0:T(8,128)(2,1)} %get-tuple-element.33), channel_id=1, source_target_pairs={{0,24},{4,28},{8,16},{12,20},{16,8},{20,12},{24,0},{28,4},{1,25},{... | collective-permute-start | bytes 737288 | tf_op jit(solution)/shard_map/ppermute | solution.py:379
  19.1 2.5 %copy-done = bf16[40,64,1024]{2,1,0:T(8,128)(2,1)S(1)} copy-done((bf16[40,64,1024]{2,1,0:T(8,128)(2,1)S(1)}, bf16[40,64,1024]{2,1,0:T(8,128)(2,1)}, u32[]{:S(2)}) %copy-start) | copy-done | bytes 5242904
  21.6 2.5 %copy-done.1 = bf16[40,64,1024]{2,1,0:T(8,128)(2,1)S(1)} copy-done((bf16[40,64,1024]{2,1,0:T(8,128)(2,1)S(1)}, bf16[40,64,1024]{2,1,0:T(8,128)(2,1)}, u32[]{:S(2)}) %copy-start.1) | copy-done | bytes 5242904
  24.9 2.9 %collective-permute-done.5.refs_2_ = bf16[40,3072]{1,0:T(8,128)(2,1)S(1)} collective-permute-done((bf16[40,3072]{1,0:T(8,128)(2,1)}, bf16[40,3072]{1,0:T(8,128)(2,1)S(1)}, u32[]{:S(2)}, u32[]{:S(2)}) %collective-permute-start.5) | collective-permute-done | bytes 245792 | tf_op jit(solution)/shard_map/ppermute | solution.py:379
  27.9 3.7 %attend.1.refs_0_ = bf16[40,1024]{1,0:T(8,128)(2,1)S(1)} custom-call(bf16[40,3072]{1,0:T(8,128)(2,1)S(1)} %get-tuple-element.30.refs_0_, bf16[40,3072]{1,0:T(8,128)(2,1)S(1)} %collective-permute-done.4.refs_1_, bf16[40,3072]{1,0:T(8,128)(2,1)S(1)} %collective-permute-done.5.refs_2_, bf16[40,3072]{1,0:T(8,128)(2,1)S(1)} %collective-permute-done.6.refs_3_, ...), custom_call_target="tpu_custom_call" | custom-call | flops 209715200 | bytes 10485760 | tf_op jit(solution)/shard_map/attend/pallas_call | solution.py:225
  31.5 1.4 %collective-permute-start.7 = (bf16[40,1024]{1,0:T(8,128)(2,1)S(1)}, bf16[40,1024]{1,0:T(8,128)(2,1)S(1)}, u32[]{:S(2)}, u32[]{:S(2)}) collective-permute-start(bf16[40,1024]{1,0:T(8,128)(2,1)S(1)} %attend.1.refs_0_), channel_id=1, source_target_pairs={{0,8},{4,12},{8,0},{12,4},{16,24},{20,28},{24,16},{28,20},{1,9},{5... | collective-permute-start | bytes 245768 | tf_op jit(solution)/shard_map/ppermute | solution.py:379
  33.8 1.3 %collective-permute-start.9 = (bf16[40,1024]{1,0:T(8,128)(2,1)S(1)}, bf16[40,1024]{1,0:T(8,128)(2,1)S(1)}, u32[]{:S(2)}, u32[]{:S(2)}) collective-permute-start(bf16[40,1024]{1,0:T(8,128)(2,1)S(1)} %attend.1.refs_0_), channel_id=1, source_target_pairs={{0,24},{4,28},{8,16},{12,20},{16,8},{20,12},{24,0},{28,4},{1,25},{... | collective-permute-start | bytes 245768 | tf_op jit(solution)/shard_map/ppermute | solution.py:379
  36.0 1.4 %collective-permute-done.8.refs_2_ = bf16[40,1024]{1,0:T(8,128)(2,1)S(1)} collective-permute-done((bf16[40,1024]{1,0:T(8,128)(2,1)S(1)}, bf16[40,1024]{1,0:T(8,128)(2,1)S(1)}, u32[]{:S(2)}, u32[]{:S(2)}) %collective-permute-start.8) | collective-permute-done | bytes 81952 | tf_op jit(solution)/shard_map/ppermute | solution.py:379
  37.4 1.7 %collective-permute-done.9.refs_3_ = bf16[40,1024]{1,0:T(8,128)(2,1)S(1)} collective-permute-done((bf16[40,1024]{1,0:T(8,128)(2,1)S(1)}, bf16[40,1024]{1,0:T(8,128)(2,1)S(1)}, u32[]{:S(2)}, u32[]{:S(2)}) %collective-permute-start.9) | collective-permute-done | bytes 81952 | tf_op jit(solution)/shard_map/ppermute | solution.py:379
  39.1 1.7 %output.1 = (bf16[40,1024]{1,0:T(8,128)(2,1)S(1)}, bf16[40,1024]{1,0:T(8,128)(2,1)S(1)}, bf16[40,1024]{1,0:T(8,128)(2,1)S(1)}, bf16[40,1024]{1,0:T(8,128)(2,1)S(1)}) custom-call(s32[3]{0:T(128)S(1)} %pad_add_fusion.place, bf16[40,1024]{1,0:T(8,128)(2,1)S(1)} %attend.1.refs_0_, bf16[40,1024]{1,0:T(8,128)(2,1)S(1)} %collective-permute-done.7.refs_1_, ...), custom_call_target="tpu_custom_call" | custom-call | flops 335544320 | bytes 2097152 | tf_op jit(solution)/shard_map/output/pallas_call | solution.py:253
  40.8 1.4 %collective-permute-start.13 = (bf16[40,1024]{1,0:T(8,128)(2,1)S(1)}, bf16[40,1024]{1,0:T(8,128)(2,1)S(1)}, u32[]{:S(2)}, u32[]{:S(2)}) collective-permute-start(bf16[40,1024]{1,0:T(8,128)(2,1)S(1)} %get-tuple-element.41), channel_id=1, source_target_pairs={{0,24},{4,28},{8,16},{12,20},{16,8},{20,12},{24,0},{28,4},{1,25},{... | collective-permute-start | bytes 245768 | tf_op jit(solution)/shard_map/ppermute | solution.py:379
  42.2 1.0 %collective-permute-start.12 = (bf16[40,1024]{1,0:T(8,128)(2,1)S(1)}, bf16[40,1024]{1,0:T(8,128)(2,1)S(1)}, u32[]{:S(2)}, u32[]{:S(2)}) collective-permute-start(bf16[40,1024]{1,0:T(8,128)(2,1)S(1)} %get-tuple-element.40), channel_id=1, source_target_pairs={{0,16},{4,20},{8,24},{12,28},{16,0},{20,4},{24,8},{28,12},{1,17},{... | collective-permute-start | bytes 245768 | tf_op jit(solution)/shard_map/ppermute | solution.py:379
  43.2 1.2 %collective-permute-start.11 = (bf16[40,1024]{1,0:T(8,128)(2,1)S(1)}, bf16[40,1024]{1,0:T(8,128)(2,1)S(1)}, u32[]{:S(2)}, u32[]{:S(2)}) collective-permute-start(bf16[40,1024]{1,0:T(8,128)(2,1)S(1)} %get-tuple-element.39), channel_id=1, source_target_pairs={{0,8},{4,12},{8,0},{12,4},{16,24},{20,28},{24,16},{28,20},{1,9},{5... | collective-permute-start | bytes 245768 | tf_op jit(solution)/shard_map/ppermute | solution.py:379
  44.4 1.9 %collective-permute-done.13 = bf16[40,1024]{1,0:T(8,128)(2,1)S(1)} collective-permute-done((bf16[40,1024]{1,0:T(8,128)(2,1)S(1)}, bf16[40,1024]{1,0:T(8,128)(2,1)S(1)}, u32[]{:S(2)}, u32[]{:S(2)}) %collective-permute-start.13) | collective-permute-done | bytes 81952 | tf_op jit(solution)/shard_map/ppermute | solution.py:379
  47.8 1.5 %collective-permute-start.14 = (bf16[40,1024]{1,0:T(8,128)(2,1)S(1)}, bf16[40,1024]{1,0:T(8,128)(2,1)S(1)}, u32[]{:S(2)}, u32[]{:S(2)}) collective-permute-start(bf16[40,1024]{1,0:T(8,128)(2,1)S(1)} %get-tuple-element.50), channel_id=1, source_target_pairs={{0,1},{1,2},{2,3},{3,0},{4,5},{5,6},{6,7},{7,4},{8,9},{9,10},{10,1... | collective-permute-start | bytes 245768 | tf_op jit(solution)/shard_map/ppermute | solution.py:382
  49.3 2.6 %collective-permute-start.15 = (bf16[40,1024]{1,0:T(8,128)(2,1)S(1)}, bf16[40,1024]{1,0:T(8,128)(2,1)S(1)}, u32[]{:S(2)}, u32[]{:S(2)}) collective-permute-start(bf16[40,1024]{1,0:T(8,128)(2,1)S(1)} %get-tuple-element.49), channel_id=1, source_target_pairs={{0,2},{1,3},{2,0},{3,1},{4,6},{5,7},{6,4},{7,5},{8,10},{9,11},{10,... | collective-permute-start | bytes 245768 | tf_op jit(solution)/shard_map/ppermute | solution.py:382
  51.9 1.3 %collective-permute-start.16 = (bf16[40,1024]{1,0:T(8,128)(2,1)S(1)}, bf16[40,1024]{1,0:T(8,128)(2,1)S(1)}, u32[]{:S(2)}, u32[]{:S(2)}) collective-permute-start(bf16[40,1024]{1,0:T(8,128)(2,1)S(1)} %get-tuple-element.48), channel_id=1, source_target_pairs={{0,3},{1,0},{2,1},{3,2},{4,7},{5,4},{6,5},{7,6},{8,11},{9,8},{10,9... | collective-permute-start | bytes 245768 | tf_op jit(solution)/shard_map/ppermute | solution.py:382
  54.1 3.7 %collective-permute-done.15.refs_2_ = bf16[40,1024]{1,0:T(8,128)(2,1)S(1)} collective-permute-done((bf16[40,1024]{1,0:T(8,128)(2,1)S(1)}, bf16[40,1024]{1,0:T(8,128)(2,1)S(1)}, u32[]{:S(2)}, u32[]{:S(2)}) %collective-permute-start.15) | collective-permute-done | bytes 81952 | tf_op jit(solution)/shard_map/ppermute | solution.py:382
  58.4 1.1 %logits.1 = (bf16[40,1024]{1,0:T(8,128)(2,1)S(1)}, f32[40,128]{1,0:T(8,128)S(1)}, bf16[40,1152]{1,0:T(8,128)(2,1)S(1)}, bf16[40,1152]{1,0:T(8,128)(2,1)S(1)}, bf16[40,1152]{1,0:T(8,128)(2,1)S(1)}) custom-call(s32[3]{0:T(128)S(1)} %pad_add_fusion.place, bf16[40,1024]{1,0:T(8,128)(2,1)S(1)} %get-tuple-element.51.refs_0_, ...), custom_call_target="tpu_custom_call" | custom-call | flops 83886080 | bytes 2097152 | tf_op jit(solution)/shard_map/logits/pallas_call | solution.py:314
  59.5 2.2 %collective-permute-start.17 = (bf16[40,1152]{1,0:T(8,128)(2,1)S(1)}, bf16[40,1152]{1,0:T(8,128)(2,1)S(1)}, u32[]{:S(2)}, u32[]{:S(2)}) collective-permute-start(bf16[40,1152]{1,0:T(8,128)(2,1)S(1)} %get-tuple-element.45), channel_id=1, source_target_pairs={{0,1},{1,2},{2,3},{3,0},{4,5},{5,6},{6,7},{7,4},{8,9},{9,10},{10,1... | collective-permute-start | bytes 276488 | tf_op jit(solution)/shard_map/ppermute | solution.py:382
  61.7 1.4 %collective-permute-start.18 = (bf16[40,1152]{1,0:T(8,128)(2,1)S(1)}, bf16[40,1152]{1,0:T(8,128)(2,1)S(1)}, u32[]{:S(2)}, u32[]{:S(2)}) collective-permute-start(bf16[40,1152]{1,0:T(8,128)(2,1)S(1)} %get-tuple-element.46), channel_id=1, source_target_pairs={{0,2},{1,3},{2,0},{3,1},{4,6},{5,7},{6,4},{7,5},{8,10},{9,11},{10,... | collective-permute-start | bytes 276488 | tf_op jit(solution)/shard_map/ppermute | solution.py:382
  63.1 1.1 %collective-permute-start.19 = (bf16[40,1152]{1,0:T(8,128)(2,1)S(1)}, bf16[40,1152]{1,0:T(8,128)(2,1)S(1)}, u32[]{:S(2)}, u32[]{:S(2)}) collective-permute-start(bf16[40,1152]{1,0:T(8,128)(2,1)S(1)} %get-tuple-element.47), channel_id=1, source_target_pairs={{0,3},{1,0},{2,1},{3,2},{4,7},{5,4},{6,5},{7,6},{8,11},{9,8},{10,9... | collective-permute-start | bytes 276488 | tf_op jit(solution)/shard_map/ppermute | solution.py:382
  64.1 1.8 %collective-permute-done.17.refs_0_ = bf16[40,1152]{1,0:T(8,128)(2,1)S(1)} collective-permute-done((bf16[40,1152]{1,0:T(8,128)(2,1)S(1)}, bf16[40,1152]{1,0:T(8,128)(2,1)S(1)}, u32[]{:S(2)}, u32[]{:S(2)}) %collective-permute-start.17) | collective-permute-done | bytes 92192 | tf_op jit(solution)/shard_map/ppermute | solution.py:382
  65.9 2.1 %collective-permute-done.18.refs_1_ = bf16[40,1152]{1,0:T(8,128)(2,1)S(1)} collective-permute-done((bf16[40,1152]{1,0:T(8,128)(2,1)S(1)}, bf16[40,1152]{1,0:T(8,128)(2,1)S(1)}, u32[]{:S(2)}, u32[]{:S(2)}) %collective-permute-start.18) | collective-permute-done | bytes 92192 | tf_op jit(solution)/shard_map/ppermute | solution.py:382
  68.6 1.4 %finish.1 = (bf16[40,4096]{1,0:T(8,128)(2,1)}, f32[40,64]{1,0:T(8,128)}) custom-call(s32[3]{0:T(128)S(1)} %pad_add_fusion.place, bf16[40,1024]{1,0:T(8,128)(2,1)S(1)} %get-tuple-element.43.own_stream, f32[40,128]{1,0:T(8,128)S(1)} %get-tuple-element.44.own_tail, bf16[40,1152]{1,0:T(8,128)(2,1)S(1)} %collective-permute-done.17.refs_0_, ...), custom_call_target="tpu_custom_call" | custom-call | tf_op jit(solution)/shard_map/finish/pallas_call | solution.py:347
  (44 shorter events, 9.2 us)
Async XLA Ops:
  0.6 12.2 %copy-start.7 = (f32[4096]{0:T(1024)S(1)}, f32[4096]{0:T(1024)}, u32[]{:S(2)}) copy-start(f32[4096]{0:T(1024)} %param.11) | copy-start | bytes 49156
  0.6 12.2 %collective-permute-start.3 = (bf16[1536,1024]{1,0:T(8,128)(2,1)}, bf16[1536,1024]{1,0:T(8,128)(2,1)S(1)}, u32[]{:S(2)}, u32[]{:S(2)}) collective-permute-start(bf16[1536,1024]{1,0:T(8,128)(2,1)} %bitcast.26), channel_id=1, source_target_pairs={{0,4},{4,0},{8,12},{12,8},{16,20},{20,16},{24,28},{28,24},{1,5},{5... | collective-permute-start | bytes 9437192 | tf_op jit(solution)/shard_map/ppermute | solution.py:385
  1.2 33.9 %collective-permute-start.10 = (bf16[1024,512]{1,0:T(8,128)(2,1)}, bf16[1024,512]{1,0:T(8,128)(2,1)}, u32[]{:S(2)}, u32[]{:S(2)}) collective-permute-start(bf16[1024,512]{1,0:T(8,128)(2,1)} %refs_4_.3), channel_id=1, source_target_pairs={{0,4},{4,0},{8,12},{12,8},{16,20},{20,16},{24,28},{28,24},{1,5},{5... | collective-permute-start | bytes 3145736 | tf_op jit(solution)/shard_map/ppermute | solution.py:385
  1.4 1.0 %copy-start.4 = (bf16[40,4096]{1,0:T(8,128)(2,1)S(1)}, bf16[40,4096]{1,0:T(8,128)(2,1)}, u32[]{:S(2)}) copy-start(bf16[40,4096]{1,0:T(8,128)(2,1)} %refs_4_.2) | copy-start | bytes 983044
  3.0 6.7 %collective-permute-start = (bf16[40,1024]{1,0:T(8,128)(2,1)S(1)}, bf16[40,1024]{1,0:T(8,128)(2,1)S(1)}, u32[]{:S(2)}, u32[]{:S(2)}) collective-permute-start(bf16[40,1024]{1,0:T(8,128)(2,1)S(1)} %get-tuple-element.26), channel_id=1, source_target_pairs={{0,8},{4,12},{8,0},{12,4},{16,24},{20,28},{24,16},{28,20},{1,9},{5... | collective-permute-start | bytes 245768 | tf_op jit(solution)/shard_map/ppermute | solution.py:379
  6.0 5.2 %collective-permute-start.1 = (bf16[40,1024]{1,0:T(8,128)(2,1)S(1)}, bf16[40,1024]{1,0:T(8,128)(2,1)S(1)}, u32[]{:S(2)}, u32[]{:S(2)}) collective-permute-start(bf16[40,1024]{1,0:T(8,128)(2,1)S(1)} %get-tuple-element.27), channel_id=1, source_target_pairs={{0,16},{4,20},{8,24},{12,28},{16,0},{20,4},{24,8},{28,12},{1,17},{... | collective-permute-start | bytes 245768 | tf_op jit(solution)/shard_map/ppermute | solution.py:379
  7.5 5.3 %collective-permute-start.2 = (bf16[40,1024]{1,0:T(8,128)(2,1)S(1)}, bf16[40,1024]{1,0:T(8,128)(2,1)S(1)}, u32[]{:S(2)}, u32[]{:S(2)}) collective-permute-start(bf16[40,1024]{1,0:T(8,128)(2,1)S(1)} %get-tuple-element.28), channel_id=1, source_target_pairs={{0,24},{4,28},{8,16},{12,20},{16,8},{20,12},{24,0},{28,4},{1,25},{... | collective-permute-start | bytes 245768 | tf_op jit(solution)/shard_map/ppermute | solution.py:379
  7.6 1.9 %copy-start.2 = (bf16[512,3,1024]{2,0,1:T(8,128)(2,1)S(1)}, bf16[512,3,1024]{2,0,1:T(8,128)(2,1)}, u32[]{:S(2)}) copy-start(bf16[512,3,1024]{2,0,1:T(8,128)(2,1)} %param.13) | copy-start | bytes 9437188
  9.4 9.6 %copy-start.10 = (s32[40]{0:T(128)S(1)}, s32[40]{0:T(128)}, u32[]{:S(2)}) copy-start(s32[40]{0:T(128)} %param.18) | copy-start | bytes 484
  15.5 9.4 %collective-permute-start.4 = (bf16[40,3072]{1,0:T(8,128)(2,1)}, bf16[40,3072]{1,0:T(8,128)(2,1)S(1)}, u32[]{:S(2)}, u32[]{:S(2)}) collective-permute-start(bf16[40,3072]{1,0:T(8,128)(2,1)} %get-tuple-element.31), channel_id=1, source_target_pairs={{0,8},{4,12},{8,0},{12,4},{16,24},{20,28},{24,16},{28,20},{1,9},{5... | collective-permute-start | bytes 737288 | tf_op jit(solution)/shard_map/ppermute | solution.py:379
  16.1 11.8 %collective-permute-start.5 = (bf16[40,3072]{1,0:T(8,128)(2,1)}, bf16[40,3072]{1,0:T(8,128)(2,1)S(1)}, u32[]{:S(2)}, u32[]{:S(2)}) collective-permute-start(bf16[40,3072]{1,0:T(8,128)(2,1)} %get-tuple-element.32), channel_id=1, source_target_pairs={{0,16},{4,20},{8,24},{12,28},{16,0},{20,4},{24,8},{28,12},{1,17},{... | collective-permute-start | bytes 737288 | tf_op jit(solution)/shard_map/ppermute | solution.py:379
  16.8 11.0 %collective-permute-start.6 = (bf16[40,3072]{1,0:T(8,128)(2,1)}, bf16[40,3072]{1,0:T(8,128)(2,1)S(1)}, u32[]{:S(2)}, u32[]{:S(2)}) collective-permute-start(bf16[40,3072]{1,0:T(8,128)(2,1)} %get-tuple-element.33), channel_id=1, source_target_pairs={{0,24},{4,28},{8,16},{12,20},{16,8},{20,12},{24,0},{28,4},{1,25},{... | collective-permute-start | bytes 737288 | tf_op jit(solution)/shard_map/ppermute | solution.py:379
  19.1 2.5 %copy-start = (bf16[40,64,1024]{2,1,0:T(8,128)(2,1)S(1)}, bf16[40,64,1024]{2,1,0:T(8,128)(2,1)}, u32[]{:S(2)}) copy-start(bf16[40,64,1024]{2,1,0:T(8,128)(2,1)} %param.16) | copy-start | bytes 15728644
  21.6 2.5 %copy-start.1 = (bf16[40,64,1024]{2,1,0:T(8,128)(2,1)S(1)}, bf16[40,64,1024]{2,1,0:T(8,128)(2,1)}, u32[]{:S(2)}) copy-start(bf16[40,64,1024]{2,1,0:T(8,128)(2,1)} %param.17) | copy-start | bytes 15728644
  24.1 3.7 %copy-start.5 = (bf16[40,4096]{1,0:T(8,128)(2,1)S(1)}, bf16[40,4096]{1,0:T(8,128)(2,1)}, u32[]{:S(2)}) copy-start(bf16[40,4096]{1,0:T(8,128)(2,1)} %refs_4_.2) | copy-start | bytes 983044
  27.8 11.3 %copy-start.6 = (bf16[1024,512]{1,0:T(8,128)(2,1)S(1)}, bf16[1024,512]{1,0:T(8,128)(2,1)}, u32[]{:S(2)}) copy-start(bf16[1024,512]{1,0:T(8,128)(2,1)} %refs_4_.3) | copy-start | bytes 3145732
  27.8 25.4 %copy-start.9 = (s32[40,2]{0,1:T(2,128)S(1)}, s32[40,2]{0,1:T(2,128)}, u32[]{:S(2)}) copy-start(s32[40,2]{0,1:T(2,128)} %param.19) | copy-start | bytes 964
  27.8 30.6 %copy-start.3 = (bf16[1024,1024]{1,0:T(8,128)(2,1)S(1)}, bf16[1024,1024]{1,0:T(8,128)(2,1)}, u32[]{:S(2)}) copy-start(bf16[1024,1024]{1,0:T(8,128)(2,1)} %refs_6_.1) | copy-start | bytes 6291460
  27.8 30.6 %copy-start.8 = (f32[4096]{0:T(1024)S(1)}, f32[4096]{0:T(1024)}, u32[]{:S(2)}) copy-start(f32[4096]{0:T(1024)} %param.12) | copy-start | bytes 49156
  31.5 4.5 %collective-permute-start.7 = (bf16[40,1024]{1,0:T(8,128)(2,1)S(1)}, bf16[40,1024]{1,0:T(8,128)(2,1)S(1)}, u32[]{:S(2)}, u32[]{:S(2)}) collective-permute-start(bf16[40,1024]{1,0:T(8,128)(2,1)S(1)} %attend.1.refs_0_), channel_id=1, source_target_pairs={{0,8},{4,12},{8,0},{12,4},{16,24},{20,28},{24,16},{28,20},{1,9},{5... | collective-permute-start | bytes 245768 | tf_op jit(solution)/shard_map/ppermute | solution.py:379
  33.0 4.4 %collective-permute-start.8 = (bf16[40,1024]{1,0:T(8,128)(2,1)S(1)}, bf16[40,1024]{1,0:T(8,128)(2,1)S(1)}, u32[]{:S(2)}, u32[]{:S(2)}) collective-permute-start(bf16[40,1024]{1,0:T(8,128)(2,1)S(1)} %attend.1.refs_0_), channel_id=1, source_target_pairs={{0,16},{4,20},{8,24},{12,28},{16,0},{20,4},{24,8},{28,12},{1,17},{... | collective-permute-start | bytes 245768 | tf_op jit(solution)/shard_map/ppermute | solution.py:379
  33.8 5.3 %collective-permute-start.9 = (bf16[40,1024]{1,0:T(8,128)(2,1)S(1)}, bf16[40,1024]{1,0:T(8,128)(2,1)S(1)}, u32[]{:S(2)}, u32[]{:S(2)}) collective-permute-start(bf16[40,1024]{1,0:T(8,128)(2,1)S(1)} %attend.1.refs_0_), channel_id=1, source_target_pairs={{0,24},{4,28},{8,16},{12,20},{16,8},{20,12},{24,0},{28,4},{1,25},{... | collective-permute-start | bytes 245768 | tf_op jit(solution)/shard_map/ppermute | solution.py:379
  40.8 5.4 %collective-permute-start.13 = (bf16[40,1024]{1,0:T(8,128)(2,1)S(1)}, bf16[40,1024]{1,0:T(8,128)(2,1)S(1)}, u32[]{:S(2)}, u32[]{:S(2)}) collective-permute-start(bf16[40,1024]{1,0:T(8,128)(2,1)S(1)} %get-tuple-element.41), channel_id=1, source_target_pairs={{0,24},{4,28},{8,16},{12,20},{16,8},{20,12},{24,0},{28,4},{1,25},{... | collective-permute-start | bytes 245768 | tf_op jit(solution)/shard_map/ppermute | solution.py:379
  42.2 4.9 %collective-permute-start.12 = (bf16[40,1024]{1,0:T(8,128)(2,1)S(1)}, bf16[40,1024]{1,0:T(8,128)(2,1)S(1)}, u32[]{:S(2)}, u32[]{:S(2)}) collective-permute-start(bf16[40,1024]{1,0:T(8,128)(2,1)S(1)} %get-tuple-element.40), channel_id=1, source_target_pairs={{0,16},{4,20},{8,24},{12,28},{16,0},{20,4},{24,8},{28,12},{1,17},{... | collective-permute-start | bytes 245768 | tf_op jit(solution)/shard_map/ppermute | solution.py:379
  43.2 4.4 %collective-permute-start.11 = (bf16[40,1024]{1,0:T(8,128)(2,1)S(1)}, bf16[40,1024]{1,0:T(8,128)(2,1)S(1)}, u32[]{:S(2)}, u32[]{:S(2)}) collective-permute-start(bf16[40,1024]{1,0:T(8,128)(2,1)S(1)} %get-tuple-element.39), channel_id=1, source_target_pairs={{0,8},{4,12},{8,0},{12,4},{16,24},{20,28},{24,16},{28,20},{1,9},{5... | collective-permute-start | bytes 245768 | tf_op jit(solution)/shard_map/ppermute | solution.py:379
  47.8 6.3 %collective-permute-start.14 = (bf16[40,1024]{1,0:T(8,128)(2,1)S(1)}, bf16[40,1024]{1,0:T(8,128)(2,1)S(1)}, u32[]{:S(2)}, u32[]{:S(2)}) collective-permute-start(bf16[40,1024]{1,0:T(8,128)(2,1)S(1)} %get-tuple-element.50), channel_id=1, source_target_pairs={{0,1},{1,2},{2,3},{3,0},{4,5},{5,6},{6,7},{7,4},{8,9},{9,10},{10,1... | collective-permute-start | bytes 245768 | tf_op jit(solution)/shard_map/ppermute | solution.py:382
  49.3 8.5 %collective-permute-start.15 = (bf16[40,1024]{1,0:T(8,128)(2,1)S(1)}, bf16[40,1024]{1,0:T(8,128)(2,1)S(1)}, u32[]{:S(2)}, u32[]{:S(2)}) collective-permute-start(bf16[40,1024]{1,0:T(8,128)(2,1)S(1)} %get-tuple-element.49), channel_id=1, source_target_pairs={{0,2},{1,3},{2,0},{3,1},{4,6},{5,7},{6,4},{7,5},{8,10},{9,11},{10,... | collective-permute-start | bytes 245768 | tf_op jit(solution)/shard_map/ppermute | solution.py:382
  51.9 6.5 %collective-permute-start.16 = (bf16[40,1024]{1,0:T(8,128)(2,1)S(1)}, bf16[40,1024]{1,0:T(8,128)(2,1)S(1)}, u32[]{:S(2)}, u32[]{:S(2)}) collective-permute-start(bf16[40,1024]{1,0:T(8,128)(2,1)S(1)} %get-tuple-element.48), channel_id=1, source_target_pairs={{0,3},{1,0},{2,1},{3,2},{4,7},{5,4},{6,5},{7,6},{8,11},{9,8},{10,9... | collective-permute-start | bytes 245768 | tf_op jit(solution)/shard_map/ppermute | solution.py:382
  59.5 6.4 %collective-permute-start.17 = (bf16[40,1152]{1,0:T(8,128)(2,1)S(1)}, bf16[40,1152]{1,0:T(8,128)(2,1)S(1)}, u32[]{:S(2)}, u32[]{:S(2)}) collective-permute-start(bf16[40,1152]{1,0:T(8,128)(2,1)S(1)} %get-tuple-element.45), channel_id=1, source_target_pairs={{0,1},{1,2},{2,3},{3,0},{4,5},{5,6},{6,7},{7,4},{8,9},{9,10},{10,1... | collective-permute-start | bytes 276488 | tf_op jit(solution)/shard_map/ppermute | solution.py:382
  61.7 6.3 %collective-permute-start.18 = (bf16[40,1152]{1,0:T(8,128)(2,1)S(1)}, bf16[40,1152]{1,0:T(8,128)(2,1)S(1)}, u32[]{:S(2)}, u32[]{:S(2)}) collective-permute-start(bf16[40,1152]{1,0:T(8,128)(2,1)S(1)} %get-tuple-element.46), channel_id=1, source_target_pairs={{0,2},{1,3},{2,0},{3,1},{4,6},{5,7},{6,4},{7,5},{8,10},{9,11},{10,... | collective-permute-start | bytes 276488 | tf_op jit(solution)/shard_map/ppermute | solution.py:382
  63.1 5.5 %collective-permute-start.19 = (bf16[40,1152]{1,0:T(8,128)(2,1)S(1)}, bf16[40,1152]{1,0:T(8,128)(2,1)S(1)}, u32[]{:S(2)}, u32[]{:S(2)}) collective-permute-start(bf16[40,1152]{1,0:T(8,128)(2,1)S(1)} %get-tuple-element.47), channel_id=1, source_target_pairs={{0,3},{1,0},{2,1},{3,2},{4,7},{5,4},{6,5},{7,6},{8,11},{9,8},{10,9... | collective-permute-start | bytes 276488 | tf_op jit(solution)/shard_map/ppermute | solution.py:382

commit v3 on v2

--- a/solution.py
+++ b/solution.py
@@ -11,13 +11,15 @@
 BEAMS = 20
 BLOCK = 128
 CORES = 2
+PIECES = 4
 LOW = -3e38
+LOG2E = 1.4426950408889634
 BF = jnp.bfloat16
 F32 = jnp.float32
 
 VM = pl.BlockSpec(memory_space=pltpu.VMEM)
 SM = pl.BlockSpec(memory_space=pltpu.SMEM)
-ANY = pl.BlockSpec(memory_space=pl.ANY)
+HB = pl.BlockSpec(memory_space=pltpu.HBM)
 
 
 def shape(dims, kind):
@@ -50,27 +52,26 @@
     rows, features = tokens.shape
     return pl.pallas_call(
         functools.partial(split_kernel, chips),
-        in_specs=[SM, ANY],
+        in_specs=[SM, HB],
         out_specs=[VM] * (chips + 1),
         out_shape=[shape((rows, features // chips), tokens.dtype)] * (chips + 1),
         scratch_shapes=[pltpu.SemaphoreType.DMA((chips + 1,))],
         compiler_params=params(4),
         cost_estimate=cost(0, 4 * tokens.size),
         name="split",
-    )(place, tokens)
+    )(place, in_hbm(tokens))
 
 
 def fetch_kernel(count, *refs):
     sources, targets, sems = refs[:count], refs[count : 2 * count], refs[2 * count]
     copies = []
     for i in range(count):
-        pieces = 4 if sources[i].shape[0] % 32 == 0 else 1
-        size = sources[i].shape[0] // pieces
-        for n in range(pieces):
+        size = targets[i].shape[0] // PIECES
+        for n in range(PIECES):
             part = pl.ds(n * size, size)
             copies.append(
                 pltpu.make_async_copy(
-                    sources[i].at[part], targets[i].at[part], sems.at[4 * i + n]
+                    sources[i].at[part], targets[i].at[part], sems.at[PIECES * i + n]
                 )
             )
     for copy in copies:
@@ -83,75 +84,120 @@
     count = len(sources)
     return pl.pallas_call(
         functools.partial(fetch_kernel, count),
-        in_specs=[ANY] * count,
+        in_specs=[HB] * count,
         out_specs=[VM] * count,
         out_shape=[shape(source.shape, source.dtype) for source in sources],
-        scratch_shapes=[pltpu.SemaphoreType.DMA((4 * count,))],
-        compiler_params=params(16),
+        scratch_shapes=[pltpu.SemaphoreType.DMA((PIECES * count,))],
+        compiler_params=params(2),
         cost_estimate=cost(0, sum(4 * source.size for source in sources)),
         name=name,
-    )(*sources)
-
-
-def project_kernel(chips, place, *refs):
+    )(*[in_hbm(source) for source in sources])
+
+
+def in_hbm(value):
+    return pltpu.with_memory_space_constraint(value, pltpu.HBM)
+
+
+def scale_pieces(place, pieces, gain, scratch):
+    rows, width = pieces[0].shape
+    scaled = gain[:, pl.ds(pl.multiple_of(place[2] * width, width), width)]
+    for k, piece in enumerate(pieces):
+        scratch[k * rows : (k + 1) * rows, :] = piece[...].astype(F32) * scaled
+    half = width // CORES
+    own = pl.ds(pl.multiple_of(place[0] * half, half), half)
+    other = pl.ds(pl.multiple_of((1 - place[0]) * half, half), half)
+    return scratch[:, own].astype(BF), scratch[:, other].astype(BF)
+
+
+def multiply(own_x, other_x, own_w, other_w, kinds, outs):
+    rows = outs[0].shape[0]
+    depth, columns = own_w.shape[0] // 3, own_w.shape[1]
+    tile = min(512, columns)
+    for index, kind in enumerate(kinds):
+        at = slice(kind * depth, (kind + 1) * depth)
+        for n in range(columns // tile):
+            to = slice(n * tile, (n + 1) * tile)
+            total = jnp.dot(own_x, own_w[at, to], preferred_element_type=F32) + jnp.dot(
+                other_x, other_w[at, to], preferred_element_type=F32
+            )
+            where = slice(index * columns + n * tile, index * columns + (n + 1) * tile)
+            for k, out in enumerate(outs):
+                out[:, where] = total[k * rows : (k + 1) * rows].astype(BF)
+
+
+def query_kernel(chips, place, *refs):
     pieces, (gain, own_w, other_w) = refs[:chips], refs[chips : chips + 3]
-    outs, scratch = refs[chips + 3 : 2 * chips + 3], refs[-1]
-    rows, width = pieces[0].shape
-    depth = own_w.shape[0] // 3
-    columns = own_w.shape[1]
-    scaled = gain[:, pl.ds(pl.multiple_of(place[2] * width, width), width)]
-    for k in range(chips):
-        scratch[k * rows : (k + 1) * rows, :] = pieces[k][...].astype(F32) * scaled
-    own_at = pl.multiple_of(place[0] * depth, depth)
-    other_at = pl.multiple_of((1 - place[0]) * depth, depth)
-    own_x = scratch[:, pl.ds(own_at, depth)].astype(BF)
-    other_x = scratch[:, pl.ds(other_at, depth)].astype(BF)
-    tile = min(512, columns)
-    for i in range(3):
-        for n in range(columns // tile):
-            at = slice(n * tile, (n + 1) * tile)
-            total = jnp.dot(
-                own_x, own_w[i * depth : (i + 1) * depth, at], preferred_element_type=F32
-            ) + jnp.dot(
-                other_x, other_w[i * depth : (i + 1) * depth, at], preferred_element_type=F32
-            )
-            to = slice(i * columns + n * tile, i * columns + (n + 1) * tile)
-            for k in range(chips):
-                outs[k][:, to] = total[k * rows : (k + 1) * rows].astype(BF)
-
-
-def project(place, pieces, gain, own_w, other_w):
+    outs, (own_x, other_x, scratch) = refs[chips + 3 : 2 * chips + 3], refs[-3:]
+    own, other = scale_pieces(place, pieces, gain, scratch)
+    own_x[...] = own
+    other_x[...] = other
+    multiply(own, other, own_w, other_w, (0,), outs)
+
+
+def project_query(place, pieces, gain, own_w, other_w):
     chips = len(pieces)
     rows, width = pieces[0].shape
     columns = own_w.shape[1]
     return pl.pallas_call(
-        functools.partial(project_kernel, chips),
+        functools.partial(query_kernel, chips),
         in_specs=[SM] + [VM] * (chips + 3),
+        out_specs=[VM] * (chips + 2),
+        out_shape=[shape((rows, columns), BF)] * chips
+        + [shape((chips * rows, width // CORES), BF)] * 2,
+        scratch_shapes=[pltpu.VMEM((chips * rows, width), F32)],
+        compiler_params=params(8),
+        cost_estimate=cost(2 * chips * rows * width * columns, 4 * width * columns),
+        name="query",
+    )(place, *pieces, gain, own_w, other_w)
+
+
+def pair_kernel(own_x, other_x, own_w, other_w, *outs):
+    multiply(own_x[...], other_x[...], own_w, other_w, (1, 2), outs)
+
+
+def project_pair(own_x, other_x, own_w, other_w, chips):
+    rows = own_x.shape[0] // chips
+    columns = own_w.shape[1]
+    return pl.pallas_call(
+        pair_kernel,
+        in_specs=[VM] * 4,
         out_specs=[VM] * chips,
-        out_shape=[shape((rows, 3 * columns), BF)] * chips,
-        scratch_shapes=[pltpu.VMEM((chips * rows, width), F32)],
-        compiler_params=params(12),
-        cost_estimate=cost(2 * chips * rows * width * 3 * columns, 4 * own_w.size),
-        name="project",
-    )(place, *pieces, gain, own_w, other_w)
+        out_shape=[shape((rows, 2 * columns), BF)] * chips,
+        compiler_params=params(8),
+        cost_estimate=cost(4 * own_x.size * 2 * columns, 8 * own_x.shape[1] * columns),
+        name="pair",
+    )(own_x, other_x, own_w, other_w)
+
+
+def column_of(row):
+    count = row.shape[1]
+    at = lax.broadcasted_iota(jnp.int32, (count, count), 0)
+    to = lax.broadcasted_iota(jnp.int32, (count, count), 1)
+    return jnp.sum(jnp.where(at == to, row.astype(F32), 0.0), axis=1, keepdims=True).astype(
+        jnp.int32
+    )
+
+
+def row_factor(tokens):
+    value = tokens[...].astype(F32)
+    return lax.rsqrt(jnp.mean(value * value, axis=1, keepdims=True) + 1e-06)
 
 
 def attend_kernel(count, *refs):
     parts = refs[:count]
-    tokens, source, keys, values, out, scores, sums = refs[count:]
-    rows, three = parts[0].shape
-    width = three // 3
+    tokens, parents, keys, values, query, result, tops, sums, scores, weights = refs[count:]
+    rows, width = query.shape
     heads = width // HEAD
     cached = keys.shape[0] // rows
     total = parts[0][...].astype(F32)
     for part in parts[1:]:
         total += part[...].astype(F32)
-    stream = tokens[...].astype(F32)
-    factor = lax.rsqrt(jnp.mean(stream * stream, axis=1, keepdims=True) + 1e-06)
-    projected = (total * factor).astype(BF)
+    projected = (total * row_factor(tokens)).astype(BF)
+    query[...] = projected
     span = BEAMS * cached
     groups = rows // BEAMS
     position = lax.broadcasted_iota(jnp.int32, (1, span), 1) // cached
+    parent_of = column_of(parents[...])
     windows = []
     for group in range(groups):
         first = group * BEAMS
@@ -160,78 +206,108 @@
     for group, (low, high) in enumerate(windows):
         for head in range(heads):
             at = slice(head * HEAD, (head + 1) * HEAD)
-            block = keys[group * span : (group + 1) * span, at]
             place = (group * heads + head) * size
             scores[place : place + high - low, :] = lax.dot_general(
                 projected[low:high, at],
-                block,
+                keys[group * span : (group + 1) * span, at],
                 (((1,), (1,)), ((), ())),
                 preferred_element_type=F32,
             )
-    unit = HEAD ** (-0.5) * 1.4426950408889634
-    news = []
+    unit = HEAD ** (-0.5) * LOG2E
+    marks = []
+    for group, (low, high) in enumerate(windows):
+        token = lax.broadcasted_iota(jnp.int32, (high - low, 1), 0) + low
+        marks.append((token >= group * BEAMS) & (token < (group + 1) * BEAMS))
+    lane = lax.broadcasted_iota(jnp.int32, (size, tops.shape[1]), 1)
     for group, (low, high) in enumerate(windows):
         first = group * BEAMS
-        bias = jnp.where(position == source[low:high] - first, 0.0, LOW)
+        parent = jnp.where(marks[group], parent_of[low:high], -1)
+        bias = jnp.where(position == parent, 0.0, LOW)
+        all_tops = jnp.zeros((high - low, tops.shape[1]), F32)
+        all_sums = all_tops
+        for head in range(heads):
+            place = (group * heads + head) * size
+            score = scores[place : place + high - low, :] * unit + bias
+            top = jnp.max(score, axis=1, keepdims=True)
+            weight = jnp.exp2(score - top)
+            mass = jnp.sum(weight, axis=1, keepdims=True)
+            weights[place : place + high - low, :] = weight
+            here = lane[: high - low] == head
+            all_tops = jnp.where(here, top, all_tops)
+            all_sums = jnp.where(here, mass, all_sums)
+        for target, value in ((tops, all_tops), (sums, all_sums)):
+            if low == first:
+                target[low:high, :] = value
+            else:
+                target[low:high, :] = jnp.where(marks[group], value, target[low:high, :])
+    for group, (low, high) in enumerate(windows):
         for head in range(heads):
             at = slice(head * HEAD, (head + 1) * HEAD)
-            key_at = slice(width + head * HEAD, width + (head + 1) * HEAD)
             place = (group * heads + head) * size
-            score = scores[place : place + high - low, :] * unit + bias
-            new_score = (
-                jnp.sum(
-                    projected[low:high, at].astype(F32) * projected[low:high, key_at].astype(F32),
-                    axis=1,
-                    keepdims=True,
-                )
-                * unit
+            value = jnp.dot(
+                weights[place : place + high - low, :].astype(BF),
+                values[group * span : (group + 1) * span, at],
+                preferred_element_type=F32,
             )
-            top = jnp.maximum(jnp.max(score, axis=1, keepdims=True), new_score)
-            weight = jnp.exp2(score - top)
-            new_weight = jnp.exp2(new_score - top)
-            scale = 1.0 / (jnp.sum(weight, axis=1, keepdims=True) + new_weight)
-            sums[place : place + high - low, :] = weight.astype(BF).astype(F32)
-            news.append((new_weight, scale))
-    for group, (low, high) in enumerate(windows):
-        first = group * BEAMS
-        token = lax.broadcasted_iota(jnp.int32, (high - low, 1), 0) + low
-        mine = (token >= first) & (token < first + BEAMS)
-        for head in range(heads):
-            at = slice(head * HEAD, (head + 1) * HEAD)
-            value_at = slice(2 * width + head * HEAD, 2 * width + (head + 1) * HEAD)
-            place = (group * heads + head) * size
-            new_weight, scale = news[group * heads + head]
-            result = (
-                jnp.dot(
-                    sums[place : place + high - low, :].astype(BF),
-                    values[group * span : (group + 1) * span, at],
-                    preferred_element_type=F32,
-                )
-                + new_weight.astype(BF).astype(F32) * projected[low:high, value_at].astype(F32)
-            ) * scale
-            if low == first:
-                out[low:high, at] = result.astype(out.dtype)
+            if low == group * BEAMS:
+                result[low:high, at] = value
             else:
-                out[low:high, at] = jnp.where(
-                    mine, result, out[low:high, at].astype(F32)
-                ).astype(out.dtype)
-
-
-def attend(parts, tokens, source, keys, values):
-    rows, three = parts[0].shape
-    width = three // 3
+                result[low:high, at] = jnp.where(marks[group], value, result[low:high, at])
+
+
+def attend(parts, tokens, parents, keys, values):
+    rows, width = parts[0].shape
     cached = keys.shape[0] // rows
     stack = rows // BEAMS * (width // HEAD) * (-(-BEAMS // 8) * 8 + 8)
     return pl.pallas_call(
         functools.partial(attend_kernel, len(parts)),
         in_specs=[VM] * (len(parts) + 4),
-        out_specs=VM,
-        out_shape=shape((rows, width), BF),
+        out_specs=[VM] * 4,
+        out_shape=[
+            shape((rows, width), BF),
+            shape((rows, width), F32),
+            shape((rows, HEAD), F32),
+            shape((rows, HEAD), F32),
+        ],
         scratch_shapes=[pltpu.VMEM((stack, BEAMS * cached), F32)] * 2,
         compiler_params=params(14),
         cost_estimate=cost(4 * rows * BEAMS * cached * width, 4 * keys.size),
         name="attend",
-    )(*parts, tokens, source, keys, values)
+    )(*parts, tokens, parents, keys, values)
+
+
+def merge_kernel(count, *refs):
+    parts = refs[:count]
+    tokens, query, result, tops, sums, out = refs[count:]
+    width = query.shape[1]
+    total = parts[0][...].astype(F32)
+    for part in parts[1:]:
+        total += part[...].astype(F32)
+    projected = (total * row_factor(tokens)).astype(BF).astype(F32)
+    product = query[...].astype(F32) * projected[:, :width]
+    unit = HEAD ** (-0.5) * LOG2E
+    for head in range(width // HEAD):
+        at = slice(head * HEAD, (head + 1) * HEAD)
+        score = jnp.sum(product[:, at], axis=1, keepdims=True) * unit
+        old = tops[:, head : head + 1]
+        top = jnp.maximum(old, score)
+        keep = jnp.exp2(old - top)
+        weight = jnp.exp2(score - top)
+        scale = 1.0 / (sums[:, head : head + 1] * keep + weight)
+        value = projected[:, width + head * HEAD : width + (head + 1) * HEAD]
+        out[:, at] = (result[:, at] * (keep * scale) + value * (weight * scale)).astype(BF)
+
+
+def merge(parts, tokens, query, result, tops, sums):
+    return pl.pallas_call(
+        functools.partial(merge_kernel, len(parts)),
+        in_specs=[VM] * (len(parts) + 5),
+        out_specs=VM,
+        out_shape=shape(query.shape, BF),
+        compiler_params=params(8),
+        cost_estimate=cost(query.size * 8, query.size * 8),
+        name="merge",
+    )(*parts, tokens, query, result, tops, sums)
 
 
 def output_kernel(chips, place, *refs):
@@ -277,8 +353,8 @@
     scaled = gain[:, pl.ds(pl.multiple_of(place[1] * width, width), width)]
     whole = jnp.dot((value * scaled).astype(BF), weight[...], preferred_element_type=F32)
     picked = []
-    for slot in range(allowed.shape[1]):
-        wanted = allowed[:, slot : slot + 1]
+    for slot in range(allowed.shape[0]):
+        wanted = column_of(allowed[slot : slot + 1, :])
         total = jnp.zeros((rows, BLOCK), F32)
         for block in range(whole.shape[1] // BLOCK):
             total = jnp.where(
@@ -309,7 +385,7 @@
 def logits(place, partials, tokens, gain, weight, allowed):
     count = len(partials)
     rows, width = tokens.shape
-    share = allowed.shape[1] * BLOCK // count
+    share = allowed.shape[0] * BLOCK // count
     wide = (share + 1 + BLOCK) // BLOCK * BLOCK
     return pl.pallas_call(
         functools.partial(logits_kernel, count),
@@ -384,26 +460,32 @@
     def to_core(value):
         return lax.ppermute(value, "dp", [(i, i ^ 1) for i in range(dp)])
 
+    def spread(values):
+        return list(values[:1]) + [to_chip(values[k], k) for k in range(1, chips)]
+
+    def after(value, *earlier):
+        return lax.optimization_barrier((value, *earlier))[0]
+
     *blocks, level_tokens = split(place, tokens, chips)
-    pieces = blocks[:1] + [to_chip(blocks[k], k) for k in range(1, chips)]
-    own_qkv = jnp.transpose(qkv_weight, (1, 0, 2)).reshape(-1, qkv_weight.shape[2])
-    other_qkv = to_core(own_qkv)
+    all_qkv = jnp.transpose(qkv_weight, (1, 0, 2)).reshape(-1, qkv_weight.shape[2])
+    other_qkv = to_core(all_qkv)
     other_out = to_core(out_weight)
-    own_qkv, _ = lax.optimization_barrier((own_qkv, blocks[0]))
-    (own_qkv,) = fetch("fetch_qkv", own_qkv)
-
-    parts = list(project(place, pieces, attn_gain[None], own_qkv, other_qkv))
+    pieces = spread(blocks)
     head_width = key_cache.shape[2]
     caches = (key_cache.reshape(-1, head_width), value_cache.reshape(-1, head_width))
-    caches, _ = lax.optimization_barrier((caches, parts[0]))
-    keys, values = fetch("fetch_cache", *caches)
-    parts = parts[:1] + [to_chip(parts[k], k) for k in range(1, chips)]
-
-    source = jnp.arange(rows, dtype=jnp.int32) // BEAMS * BEAMS + parents
-    attended = attend(parts, tokens, source[:, None], keys, values)
-
-    pieces = [attended] + [to_chip(attended, k) for k in range(1, chips)]
-    parts = list(output(place, pieces, out_weight, other_out))
+    own_qkv, keys, values = fetch("fetch", *after((all_qkv, *caches), blocks[0]))
+
+    *parts, own_x, other_x = project_query(
+        place, pieces, attn_gain[None], own_qkv, other_qkv
+    )
+    parts = spread(parts)
+    pairs = spread(project_pair(own_x, other_x, own_qkv, other_qkv, chips))
+    seen = attend(parts, tokens, parents[None], keys, values)
+    attended = merge(pairs, tokens, *seen)
+
+    pieces = spread([attended] * chips)
+    own_out, other_out = fetch("fetch_out", *after((out_weight, other_out), attended))
+    parts = list(output(place, pieces, own_out, other_out))
     parts = jnp.stack(parts[:1] + [to_chip(parts[k], k) for k in range(1, chips)])
     slices = [
         lax.dynamic_index_in_dim(parts, chip ^ ((level + m) % mp), 0, keepdims=False)
@@ -411,7 +493,7 @@
     ]
     slices = slices[:1] + [to_level(slices[m], m) for m in range(1, mp)]
     own_stream, own_tail, *others = logits(
-        place, slices, level_tokens, head_gain[None], head_weight, allowed
+        place, slices, level_tokens, head_gain[None], head_weight, allowed.T
     )
     others = [to_level(other, m + 1) for m, other in enumerate(others)]
     return tuple(finish(place, own_stream, own_tail, others, allowed.shape[1] * BLOCK // mp))

time: 70.2 us -> 70.5 us (level)
  local copies, waits for them, and re-layouts: 8.08 us -> 0.07 us
  Pallas kernels: 12.3 us -> 17.8 us
  starting transfers between devices: 25.8 us -> 29.8 us
  waiting for transfers between devices: 22.9 us -> 21.7 us
    unnamed x23 -> x12, local copies, waits for them, and re-layouts: 7.96 us -> 0.03 us
    pallas_call x4 -> x6, Pallas kernels: 4.38 us -> 10.8 us  [the longest x2 6.6 us: fetch(): pl.pallas_call(functools.partial(fetch_kernel, count), in_specs=[HB] * co...]
    ppermute x12 -> x15, starting transfers between devices: 15.1 us -> 19 us  [to_chip(): return lax.ppermute(value, 'dp', [(i, i ^ CORES * k) for i in range(dp)])]
    ppermute x12 -> x15, waiting for transfers between devices: 13.4 us -> 12.7 us  [to_chip(): return lax.ppermute(value, 'dp', [(i, i ^ CORES * k) for i in range(dp)])]
  transfers between devices with their start and end apart: 20 -> 23, of which waited for: 15 -> 13; matrix products, arithmetic and copies ran while one was open for 0% -> 0% of each run, Pallas kernels for 12% -> 20%
where the time goes in v3:
time: 70.5 us; the launch traced here: 70.3 us
  starting transfers between devices  29.8 us (42%)
  waiting for transfers between devices  21.7 us (31%)
  Pallas kernels  17.8 us (25%)
  between operations  0.81 us (1%)
    ppermute x15, starting transfers between devices, to_chip(): return lax.ppermute(value, 'dp', [(i, i ^ CORES * k) for i in range(dp)])  19 us
    ppermute x15, waiting for transfers between devices, to_chip(): return lax.ppermute(value, 'dp', [(i, i ^ CORES * k) for i in range(dp)])  12.7 us
    ppermute x6, starting transfers between devices, to_level(): return lax.ppermute(value, 'mp', [(i, (i + m) % mp) for i in range(mp)])  10.1 us
    ppermute x6, waiting for transfers between devices, to_level(): return lax.ppermute(value, 'mp', [(i, (i + m) % mp) for i in range(mp)])  9.06 us
    pallas_call x2, Pallas kernels, fetch(): pl.pallas_call(functools.partial(fetch_kernel, count), in_specs=[HB] * co...  6.6 us
    pallas_call x1, Pallas kernels, attend(): pl.pallas_call(functools.partial(attend_kernel, len(parts)), in_specs=[VM...  3.52 us
    pallas_call x1, Pallas kernels, split(): pl.pallas_call(functools.partial(split_kernel, chips), in_specs=[SM, HB],...  1.64 us
  transfers between devices with their start and end apart: 23, of which 13 were waited for; matrix products, arithmetic and copies ran while one was open for 0% of the time, Pallas kernels for 20%

profile of v3, /device:TPU:0, one launch (start us, length us, event | category | flops | bytes accessed | tf_op | source)
XLA Modules:
  0.0 70.3 jit_solution(15497057630658141851)
XLA Ops:
  1.3 1.6 %split.1 = (bf16[40,1024]{1,0:T(8,128)(2,1)S(1)}, bf16[40,1024]{1,0:T(8,128)(2,1)S(1)}, bf16[40,1024]{1,0:T(8,128)(2,1)S(1)}, bf16[40,1024]{1,0:T(8,128)(2,1)S(1)}, bf16[40,1024]{1,0:T(8,128)(2,1)S(1)}) custom-call(s32[3]{0:T(128)S(1)} %pad_add_fusion.place, bf16[40,4096]{1,0:T(8,128)(2,1)} %refs_4_.3), custom_call_target="tpu_custom_call" | custom-call | bytes 655360 | tf_op jit(solution)/shard_map/split/pallas_call | solution.py:53
  3.0 3.0 %collective-permute-start = (bf16[40,1024]{1,0:T(8,128)(2,1)S(1)}, bf16[40,1024]{1,0:T(8,128)(2,1)S(1)}, u32[]{:S(2)}, u32[]{:S(2)}) collective-permute-start(bf16[40,1024]{1,0:T(8,128)(2,1)S(1)} %get-tuple-element.41), channel_id=1, source_target_pairs={{0,8},{4,12},{8,0},{12,4},{16,24},{20,28},{24,16},{28,20},{1,9},{5... | collective-permute-start | bytes 245768 | tf_op jit(solution)/shard_map/ppermute | solution.py:455
  6.0 1.5 %collective-permute-start.1 = (bf16[40,1024]{1,0:T(8,128)(2,1)S(1)}, bf16[40,1024]{1,0:T(8,128)(2,1)S(1)}, u32[]{:S(2)}, u32[]{:S(2)}) collective-permute-start(bf16[40,1024]{1,0:T(8,128)(2,1)S(1)} %get-tuple-element.42), channel_id=1, source_target_pairs={{0,16},{4,20},{8,24},{12,28},{16,0},{20,4},{24,8},{28,12},{1,17},{... | collective-permute-start | bytes 245768 | tf_op jit(solution)/shard_map/ppermute | solution.py:455
  7.5 5.0 %fetch.1 = (bf16[1536,1024]{1,0:T(8,128)(2,1)S(1)}, bf16[2560,1024]{1,0:T(8,128)(2,1)S(1)}, bf16[2560,1024]{1,0:T(8,128)(2,1)S(1)}) custom-call(bf16[1536,1024]{1,0:T(8,128)(2,1)} %bitcast.32, bf16[2560,1024]{1,0:T(8,128)(2,1)} %bitcast.29, bf16[2560,1024]{1,0:T(8,128)(2,1)} %bitcast.30), custom_call_target="tpu_custom_call" | custom-call | bytes 27262976 | tf_op jit(solution)/shard_map/fetch/pallas_call | solution.py:85
  12.8 1.1 %query.1 = (bf16[40,1024]{1,0:T(8,128)(2,1)S(1)}, bf16[40,1024]{1,0:T(8,128)(2,1)S(1)}, bf16[40,1024]{1,0:T(8,128)(2,1)S(1)}, bf16[40,1024]{1,0:T(8,128)(2,1)S(1...) custom-call(s32[3]{0:T(128)S(1)} %pad_add_fusion.place, bf16[40,1024]{1,0:T(8,128)(2,1)S(1)} %get-tuple-element.40.refs_0_, ...), custom_call_target="tpu_custom_call" | custom-call | flops 335544320 | bytes 4194304 | tf_op jit(solution)/shard_map/query/pallas_call | solution.py:141
  13.9 1.8 %collective-permute-start.7 = (bf16[40,1024]{1,0:T(8,128)(2,1)S(1)}, bf16[40,1024]{1,0:T(8,128)(2,1)S(1)}, u32[]{:S(2)}, u32[]{:S(2)}) collective-permute-start(bf16[40,1024]{1,0:T(8,128)(2,1)S(1)} %get-tuple-element.55), channel_id=1, source_target_pairs={{0,8},{4,12},{8,0},{12,4},{16,24},{20,28},{24,16},{28,20},{1,9},{5... | collective-permute-start | bytes 245768 | tf_op jit(solution)/shard_map/ppermute | solution.py:455
  15.7 1.5 %collective-permute-start.8 = (bf16[40,1024]{1,0:T(8,128)(2,1)S(1)}, bf16[40,1024]{1,0:T(8,128)(2,1)S(1)}, u32[]{:S(2)}, u32[]{:S(2)}) collective-permute-start(bf16[40,1024]{1,0:T(8,128)(2,1)S(1)} %get-tuple-element.56), channel_id=1, source_target_pairs={{0,16},{4,20},{8,24},{12,28},{16,0},{20,4},{24,8},{28,12},{1,17},{... | collective-permute-start | bytes 245768 | tf_op jit(solution)/shard_map/ppermute | solution.py:455
  19.0 3.0 %collective-permute-start.6 = (bf16[40,2048]{1,0:T(8,128)(2,1)S(1)}, bf16[40,2048]{1,0:T(8,128)(2,1)S(1)}, u32[]{:S(2)}, u32[]{:S(2)}) collective-permute-start(bf16[40,2048]{1,0:T(8,128)(2,1)S(1)} %get-tuple-element.53), channel_id=1, source_target_pairs={{0,24},{4,28},{8,16},{12,20},{16,8},{20,12},{24,0},{28,4},{1,25},{... | collective-permute-start | bytes 491528 | tf_op jit(solution)/shard_map/ppermute | solution.py:455
  22.2 6.2 %collective-permute-done.9.refs_3_ = bf16[40,1024]{1,0:T(8,128)(2,1)S(1)} collective-permute-done((bf16[40,1024]{1,0:T(8,128)(2,1)S(1)}, bf16[40,1024]{1,0:T(8,128)(2,1)S(1)}, u32[]{:S(2)}, u32[]{:S(2)}) %collective-permute-start.9) | collective-permute-done | bytes 81952 | tf_op jit(solution)/shard_map/ppermute | solution.py:455
  28.4 3.5 %attend.1 = (bf16[40,1024]{1,0:T(8,128)(2,1)S(1)}, f32[40,1024]{1,0:T(8,128)S(1)}, f32[40,128]{1,0:T(8,128)S(1)}, f32[40,128]{1,0:T(8,128)S(1)}) custom-call(bf16[40,1024]{1,0:T(8,128)(2,1)S(1)} %get-tuple-element.54.refs_0_, bf16[40,1024]{1,0:T(8,128)(2,1)S(1)} %collective-permute-done.7.refs_1_, bf16[40,1024]{1,0:T(8,128)(2,1)S(1)} %collective-permute-done.8.refs_2_, ...), custom_call_target="tpu_custom_call" | custom-call | flops 209715200 | bytes 10485760 | tf_op jit(solution)/shard_map/attend/pallas_call | solution.py:262
  32.6 1.1 %collective-permute-start.10 = (bf16[40,1024]{1,0:T(8,128)(2,1)S(1)}, bf16[40,1024]{1,0:T(8,128)(2,1)S(1)}, u32[]{:S(2)}, u32[]{:S(2)}) collective-permute-start(bf16[40,1024]{1,0:T(8,128)(2,1)S(1)} %merge.1.refs_0_), channel_id=1, source_target_pairs={{0,8},{4,12},{8,0},{12,4},{16,24},{20,28},{24,16},{28,20},{1,9},{5... | collective-permute-start | bytes 245768 | tf_op jit(solution)/shard_map/ppermute | solution.py:455
  33.8 1.4 %collective-permute-start.11 = (bf16[40,1024]{1,0:T(8,128)(2,1)S(1)}, bf16[40,1024]{1,0:T(8,128)(2,1)S(1)}, u32[]{:S(2)}, u32[]{:S(2)}) collective-permute-start(bf16[40,1024]{1,0:T(8,128)(2,1)S(1)} %merge.1.refs_0_), channel_id=1, source_target_pairs={{0,16},{4,20},{8,24},{12,28},{16,0},{20,4},{24,8},{28,12},{1,17},{... | collective-permute-start | bytes 245768 | tf_op jit(solution)/shard_map/ppermute | solution.py:455
  35.1 1.1 %collective-permute-start.12 = (bf16[40,1024]{1,0:T(8,128)(2,1)S(1)}, bf16[40,1024]{1,0:T(8,128)(2,1)S(1)}, u32[]{:S(2)}, u32[]{:S(2)}) collective-permute-start(bf16[40,1024]{1,0:T(8,128)(2,1)S(1)} %merge.1.refs_0_), channel_id=1, source_target_pairs={{0,24},{4,28},{8,16},{12,20},{16,8},{20,12},{24,0},{28,4},{1,25},{... | collective-permute-start | bytes 245768 | tf_op jit(solution)/shard_map/ppermute | solution.py:455
  36.2 1.6 %fetch_out.1 = (bf16[1024,512]{1,0:T(8,128)(2,1)S(1)}, bf16[1024,512]{1,0:T(8,128)(2,1)S(1)}) custom-call(bf16[1024,512]{1,0:T(8,128)(2,1)} %refs_0_, bf16[1024,512]{1,0:T(8,128)(2,1)} %collective-permute-done.13.refs_1_), custom_call_target="tpu_custom_call" | custom-call | bytes 4194304 | tf_op jit(solution)/shard_map/fetch_out/pallas_call | solution.py:85
  38.4 2.1 %collective-permute-done.12.refs_3_ = bf16[40,1024]{1,0:T(8,128)(2,1)S(1)} collective-permute-done((bf16[40,1024]{1,0:T(8,128)(2,1)S(1)}, bf16[40,1024]{1,0:T(8,128)(2,1)S(1)}, u32[]{:S(2)}, u32[]{:S(2)}) %collective-permute-start.12) | collective-permute-done | bytes 81952 | tf_op jit(solution)/shard_map/ppermute | solution.py:455
  40.5 1.0 %output.1 = (bf16[40,1024]{1,0:T(8,128)(2,1)S(1)}, bf16[40,1024]{1,0:T(8,128)(2,1)S(1)}, bf16[40,1024]{1,0:T(8,128)(2,1)S(1)}, bf16[40,1024]{1,0:T(8,128)(2,1)S(1)}) custom-call(s32[3]{0:T(128)S(1)} %pad_add_fusion.place, bf16[40,1024]{1,0:T(8,128)(2,1)S(1)} %merge.1.refs_0_, bf16[40,1024]{1,0:T(8,128)(2,1)S(1)} %collective-permute-done.10.refs_1_, ...), custom_call_target="tpu_custom_call" | custom-call | flops 335544320 | bytes 2097152 | tf_op jit(solution)/shard_map/output/pallas_call | solution.py:329
  41.5 0.9 %collective-permute-start.14 = (bf16[40,1024]{1,0:T(8,128)(2,1)S(1)}, bf16[40,1024]{1,0:T(8,128)(2,1)S(1)}, u32[]{:S(2)}, u32[]{:S(2)}) collective-permute-start(bf16[40,1024]{1,0:T(8,128)(2,1)S(1)} %get-tuple-element.69), channel_id=1, source_target_pairs={{0,8},{4,12},{8,0},{12,4},{16,24},{20,28},{24,16},{28,20},{1,9},{5... | collective-permute-start | bytes 245768 | tf_op jit(solution)/shard_map/ppermute | solution.py:455
  43.2 1.9 %collective-permute-start.16 = (bf16[40,1024]{1,0:T(8,128)(2,1)S(1)}, bf16[40,1024]{1,0:T(8,128)(2,1)S(1)}, u32[]{:S(2)}, u32[]{:S(2)}) collective-permute-start(bf16[40,1024]{1,0:T(8,128)(2,1)S(1)} %get-tuple-element.71), channel_id=1, source_target_pairs={{0,24},{4,28},{8,16},{12,20},{16,8},{20,12},{24,0},{28,4},{1,25},{... | collective-permute-start | bytes 245768 | tf_op jit(solution)/shard_map/ppermute | solution.py:455
  45.1 1.0 %collective-permute-done.14 = bf16[40,1024]{1,0:T(8,128)(2,1)S(1)} collective-permute-done((bf16[40,1024]{1,0:T(8,128)(2,1)S(1)}, bf16[40,1024]{1,0:T(8,128)(2,1)S(1)}, u32[]{:S(2)}, u32[]{:S(2)}) %collective-permute-start.14) | collective-permute-done | bytes 81952 | tf_op jit(solution)/shard_map/ppermute | solution.py:455
  46.0 0.9 %collective-permute-done.15 = bf16[40,1024]{1,0:T(8,128)(2,1)S(1)} collective-permute-done((bf16[40,1024]{1,0:T(8,128)(2,1)S(1)}, bf16[40,1024]{1,0:T(8,128)(2,1)S(1)}, u32[]{:S(2)}, u32[]{:S(2)}) %collective-permute-start.15) | collective-permute-done | bytes 81952 | tf_op jit(solution)/shard_map/ppermute | solution.py:455
  46.9 1.7 %collective-permute-done.16 = bf16[40,1024]{1,0:T(8,128)(2,1)S(1)} collective-permute-done((bf16[40,1024]{1,0:T(8,128)(2,1)S(1)}, bf16[40,1024]{1,0:T(8,128)(2,1)S(1)}, u32[]{:S(2)}, u32[]{:S(2)}) %collective-permute-start.16) | collective-permute-done | bytes 81952 | tf_op jit(solution)/shard_map/ppermute | solution.py:455
  48.6 1.6 %collective-permute-start.17 = (bf16[40,1024]{1,0:T(8,128)(2,1)S(1)}, bf16[40,1024]{1,0:T(8,128)(2,1)S(1)}, u32[]{:S(2)}, u32[]{:S(2)}) collective-permute-start(bf16[40,1024]{1,0:T(8,128)(2,1)S(1)} %get-tuple-element.80), channel_id=1, source_target_pairs={{0,1},{1,2},{2,3},{3,0},{4,5},{5,6},{6,7},{7,4},{8,9},{9,10},{10,1... | collective-permute-start | bytes 245768 | tf_op jit(solution)/shard_map/ppermute | solution.py:458
  50.3 2.6 %collective-permute-start.18 = (bf16[40,1024]{1,0:T(8,128)(2,1)S(1)}, bf16[40,1024]{1,0:T(8,128)(2,1)S(1)}, u32[]{:S(2)}, u32[]{:S(2)}) collective-permute-start(bf16[40,1024]{1,0:T(8,128)(2,1)S(1)} %get-tuple-element.79), channel_id=1, source_target_pairs={{0,2},{1,3},{2,0},{3,1},{4,6},{5,7},{6,4},{7,5},{8,10},{9,11},{10,... | collective-permute-start | bytes 245768 | tf_op jit(solution)/shard_map/ppermute | solution.py:458
  52.9 1.3 %collective-permute-start.19 = (bf16[40,1024]{1,0:T(8,128)(2,1)S(1)}, bf16[40,1024]{1,0:T(8,128)(2,1)S(1)}, u32[]{:S(2)}, u32[]{:S(2)}) collective-permute-start(bf16[40,1024]{1,0:T(8,128)(2,1)S(1)} %get-tuple-element.78), channel_id=1, source_target_pairs={{0,3},{1,0},{2,1},{3,2},{4,7},{5,4},{6,5},{7,6},{8,11},{9,8},{10,9... | collective-permute-start | bytes 245768 | tf_op jit(solution)/shard_map/ppermute | solution.py:458
  54.9 0.9 %collective-permute-done.18.refs_2_ = bf16[40,1024]{1,0:T(8,128)(2,1)S(1)} collective-permute-done((bf16[40,1024]{1,0:T(8,128)(2,1)S(1)}, bf16[40,1024]{1,0:T(8,128)(2,1)S(1)}, u32[]{:S(2)}, u32[]{:S(2)}) %collective-permute-start.18) | collective-permute-done | bytes 81952 | tf_op jit(solution)/shard_map/ppermute | solution.py:458
  55.8 2.8 %collective-permute-done.19.refs_3_ = bf16[40,1024]{1,0:T(8,128)(2,1)S(1)} collective-permute-done((bf16[40,1024]{1,0:T(8,128)(2,1)S(1)}, bf16[40,1024]{1,0:T(8,128)(2,1)S(1)}, u32[]{:S(2)}, u32[]{:S(2)}) %collective-permute-start.19) | collective-permute-done | bytes 81952 | tf_op jit(solution)/shard_map/ppermute | solution.py:458
  58.6 1.1 %logits.1 = (bf16[40,1024]{1,0:T(8,128)(2,1)S(1)}, f32[40,128]{1,0:T(8,128)S(1)}, bf16[40,1152]{1,0:T(8,128)(2,1)S(1)}, bf16[40,1152]{1,0:T(8,128)(2,1)S(1)}, bf16[40,1152]{1,0:T(8,128)(2,1)S(1)}) custom-call(s32[3]{0:T(128)S(1)} %pad_add_fusion.place, bf16[40,1024]{1,0:T(8,128)(2,1)S(1)} %get-tuple-element.81.refs_0_, ...), custom_call_target="tpu_custom_call" | custom-call | flops 83886080 | bytes 2097152 | tf_op jit(solution)/shard_map/logits/pallas_call | solution.py:390
  59.7 2.1 %collective-permute-start.20 = (bf16[40,1152]{1,0:T(8,128)(2,1)S(1)}, bf16[40,1152]{1,0:T(8,128)(2,1)S(1)}, u32[]{:S(2)}, u32[]{:S(2)}) collective-permute-start(bf16[40,1152]{1,0:T(8,128)(2,1)S(1)} %get-tuple-element.75), channel_id=1, source_target_pairs={{0,1},{1,2},{2,3},{3,0},{4,5},{5,6},{6,7},{7,4},{8,9},{9,10},{10,1... | collective-permute-start | bytes 276488 | tf_op jit(solution)/shard_map/ppermute | solution.py:458
  61.9 1.6 %collective-permute-start.21 = (bf16[40,1152]{1,0:T(8,128)(2,1)S(1)}, bf16[40,1152]{1,0:T(8,128)(2,1)S(1)}, u32[]{:S(2)}, u32[]{:S(2)}) collective-permute-start(bf16[40,1152]{1,0:T(8,128)(2,1)S(1)} %get-tuple-element.76), channel_id=1, source_target_pairs={{0,2},{1,3},{2,0},{3,1},{4,6},{5,7},{6,4},{7,5},{8,10},{9,11},{10,... | collective-permute-start | bytes 276488 | tf_op jit(solution)/shard_map/ppermute | solution.py:458
  64.3 1.8 %collective-permute-done.20.refs_0_ = bf16[40,1152]{1,0:T(8,128)(2,1)S(1)} collective-permute-done((bf16[40,1152]{1,0:T(8,128)(2,1)S(1)}, bf16[40,1152]{1,0:T(8,128)(2,1)S(1)}, u32[]{:S(2)}, u32[]{:S(2)}) %collective-permute-start.20) | collective-permute-done | bytes 92192 | tf_op jit(solution)/shard_map/ppermute | solution.py:458
  66.1 2.1 %collective-permute-done.21.refs_1_ = bf16[40,1152]{1,0:T(8,128)(2,1)S(1)} collective-permute-done((bf16[40,1152]{1,0:T(8,128)(2,1)S(1)}, bf16[40,1152]{1,0:T(8,128)(2,1)S(1)}, u32[]{:S(2)}, u32[]{:S(2)}) %collective-permute-start.21) | collective-permute-done | bytes 92192 | tf_op jit(solution)/shard_map/ppermute | solution.py:458
  69.0 1.4 %finish.1 = (bf16[40,4096]{1,0:T(8,128)(2,1)}, f32[40,64]{1,0:T(8,128)}) custom-call(s32[3]{0:T(128)S(1)} %pad_add_fusion.place, bf16[40,1024]{1,0:T(8,128)(2,1)S(1)} %get-tuple-element.73.own_stream, f32[40,128]{1,0:T(8,128)S(1)} %get-tuple-element.74.own_tail, bf16[40,1152]{1,0:T(8,128)(2,1)S(1)} %collective-permute-done.20.refs_0_, ...), custom_call_target="tpu_custom_call" | custom-call | tf_op jit(solution)/shard_map/finish/pallas_call | solution.py:423
  (39 shorter events, 7.4 us)
Async XLA Ops:
  0.6 12.2 %collective-permute-start.3 = (bf16[1536,1024]{1,0:T(8,128)(2,1)}, bf16[1536,1024]{1,0:T(8,128)(2,1)S(1)}, u32[]{:S(2)}, u32[]{:S(2)}) collective-permute-start(bf16[1536,1024]{1,0:T(8,128)(2,1)} %bitcast.31), channel_id=1, source_target_pairs={{0,4},{4,0},{8,12},{12,8},{16,20},{20,16},{24,28},{28,24},{1,5},{5... | collective-permute-start | bytes 9437192 | tf_op jit(solution)/shard_map/ppermute | solution.py:461
  1.2 35.0 %collective-permute-start.13 = (bf16[1024,512]{1,0:T(8,128)(2,1)}, bf16[1024,512]{1,0:T(8,128)(2,1)}, u32[]{:S(2)}, u32[]{:S(2)}) collective-permute-start(bf16[1024,512]{1,0:T(8,128)(2,1)} %refs_0_), channel_id=1, source_target_pairs={{0,4},{4,0},{8,12},{12,8},{16,20},{20,16},{24,28},{28,24},{1,5},{5... | collective-permute-start | bytes 3145736 | tf_op jit(solution)/shard_map/ppermute | solution.py:461
  3.0 9.6 %collective-permute-start = (bf16[40,1024]{1,0:T(8,128)(2,1)S(1)}, bf16[40,1024]{1,0:T(8,128)(2,1)S(1)}, u32[]{:S(2)}, u32[]{:S(2)}) collective-permute-start(bf16[40,1024]{1,0:T(8,128)(2,1)S(1)} %get-tuple-element.41), channel_id=1, source_target_pairs={{0,8},{4,12},{8,0},{12,4},{16,24},{20,28},{24,16},{28,20},{1,9},{5... | collective-permute-start | bytes 245768 | tf_op jit(solution)/shard_map/ppermute | solution.py:455
  6.0 6.6 %collective-permute-start.1 = (bf16[40,1024]{1,0:T(8,128)(2,1)S(1)}, bf16[40,1024]{1,0:T(8,128)(2,1)S(1)}, u32[]{:S(2)}, u32[]{:S(2)}) collective-permute-start(bf16[40,1024]{1,0:T(8,128)(2,1)S(1)} %get-tuple-element.42), channel_id=1, source_target_pairs={{0,16},{4,20},{8,24},{12,28},{16,0},{20,4},{24,8},{28,12},{1,17},{... | collective-permute-start | bytes 245768 | tf_op jit(solution)/shard_map/ppermute | solution.py:455
  7.5 5.3 %collective-permute-start.2 = (bf16[40,1024]{1,0:T(8,128)(2,1)S(1)}, bf16[40,1024]{1,0:T(8,128)(2,1)S(1)}, u32[]{:S(2)}, u32[]{:S(2)}) collective-permute-start(bf16[40,1024]{1,0:T(8,128)(2,1)S(1)} %get-tuple-element.43), channel_id=1, source_target_pairs={{0,24},{4,28},{8,16},{12,20},{16,8},{20,12},{24,0},{28,4},{1,25},{... | collective-permute-start | bytes 245768 | tf_op jit(solution)/shard_map/ppermute | solution.py:455
  7.5 5.3 %copy-start.2 = (f32[4096]{0:T(1024)S(1)}, f32[4096]{0:T(1024)}, u32[]{:S(2)}) copy-start(f32[4096]{0:T(1024)} %param.11) | copy-start | bytes 49156
  12.8 15.6 %copy-start = (bf16[40,4096]{1,0:T(8,128)(2,1)S(1)}, bf16[40,4096]{1,0:T(8,128)(2,1)}, u32[]{:S(2)}) copy-start(bf16[40,4096]{1,0:T(8,128)(2,1)} %refs_4_.3) | copy-start | bytes 983044
  12.8 15.6 %copy-start.5 = (s32[40]{0:T(128)S(1)}, s32[40]{0:T(128)}, u32[]{:S(2)}) copy-start(s32[40]{0:T(128)} %param.18) | copy-start | bytes 484
  13.9 5.0 %collective-permute-start.7 = (bf16[40,1024]{1,0:T(8,128)(2,1)S(1)}, bf16[40,1024]{1,0:T(8,128)(2,1)S(1)}, u32[]{:S(2)}, u32[]{:S(2)}) collective-permute-start(bf16[40,1024]{1,0:T(8,128)(2,1)S(1)} %get-tuple-element.55), channel_id=1, source_target_pairs={{0,8},{4,12},{8,0},{12,4},{16,24},{20,28},{24,16},{28,20},{1,9},{5... | collective-permute-start | bytes 245768 | tf_op jit(solution)/shard_map/ppermute | solution.py:455
  15.7 6.3 %collective-permute-start.8 = (bf16[40,1024]{1,0:T(8,128)(2,1)S(1)}, bf16[40,1024]{1,0:T(8,128)(2,1)S(1)}, u32[]{:S(2)}, u32[]{:S(2)}) collective-permute-start(bf16[40,1024]{1,0:T(8,128)(2,1)S(1)} %get-tuple-element.56), channel_id=1, source_target_pairs={{0,16},{4,20},{8,24},{12,28},{16,0},{20,4},{24,8},{28,12},{1,17},{... | collective-permute-start | bytes 245768 | tf_op jit(solution)/shard_map/ppermute | solution.py:455
  18.1 13.9 %collective-permute-start.4 = (bf16[40,2048]{1,0:T(8,128)(2,1)S(1)}, bf16[40,2048]{1,0:T(8,128)(2,1)S(1)}, u32[]{:S(2)}, u32[]{:S(2)}) collective-permute-start(bf16[40,2048]{1,0:T(8,128)(2,1)S(1)} %get-tuple-element.51), channel_id=1, source_target_pairs={{0,8},{4,12},{8,0},{12,4},{16,24},{20,28},{24,16},{28,20},{1,9},{5... | collective-permute-start | bytes 491528 | tf_op jit(solution)/shard_map/ppermute | solution.py:455
  18.7 13.3 %collective-permute-start.5 = (bf16[40,2048]{1,0:T(8,128)(2,1)S(1)}, bf16[40,2048]{1,0:T(8,128)(2,1)S(1)}, u32[]{:S(2)}, u32[]{:S(2)}) collective-permute-start(bf16[40,2048]{1,0:T(8,128)(2,1)S(1)} %get-tuple-element.52), channel_id=1, source_target_pairs={{0,16},{4,20},{8,24},{12,28},{16,0},{20,4},{24,8},{28,12},{1,17},{... | collective-permute-start | bytes 491528 | tf_op jit(solution)/shard_map/ppermute | solution.py:455
  19.0 13.0 %collective-permute-start.6 = (bf16[40,2048]{1,0:T(8,128)(2,1)S(1)}, bf16[40,2048]{1,0:T(8,128)(2,1)S(1)}, u32[]{:S(2)}, u32[]{:S(2)}) collective-permute-start(bf16[40,2048]{1,0:T(8,128)(2,1)S(1)} %get-tuple-element.53), channel_id=1, source_target_pairs={{0,24},{4,28},{8,16},{12,20},{16,8},{20,12},{24,0},{28,4},{1,25},{... | collective-permute-start | bytes 491528 | tf_op jit(solution)/shard_map/ppermute | solution.py:455
  22.0 6.4 %collective-permute-start.9 = (bf16[40,1024]{1,0:T(8,128)(2,1)S(1)}, bf16[40,1024]{1,0:T(8,128)(2,1)S(1)}, u32[]{:S(2)}, u32[]{:S(2)}) collective-permute-start(bf16[40,1024]{1,0:T(8,128)(2,1)S(1)} %get-tuple-element.57), channel_id=1, source_target_pairs={{0,24},{4,28},{8,16},{12,20},{16,8},{20,12},{24,0},{28,4},{1,25},{... | collective-permute-start | bytes 245768 | tf_op jit(solution)/shard_map/ppermute | solution.py:455
  31.9 26.7 %copy-start.1 = (bf16[1024,1024]{1,0:T(8,128)(2,1)S(1)}, bf16[1024,1024]{1,0:T(8,128)(2,1)}, u32[]{:S(2)}) copy-start(bf16[1024,1024]{1,0:T(8,128)(2,1)} %refs_6_.1) | copy-start | bytes 6291460
  32.0 26.7 %copy-start.3 = (f32[4096]{0:T(1024)S(1)}, f32[4096]{0:T(1024)}, u32[]{:S(2)}) copy-start(f32[4096]{0:T(1024)} %param.12) | copy-start | bytes 49156
  32.0 26.7 %copy-start.4 = (s32[40,2]{0,1:T(2,128)S(1)}, s32[40,2]{0,1:T(2,128)}, u32[]{:S(2)}) copy-start(s32[40,2]{0,1:T(2,128)} %param.19) | copy-start | bytes 964
  32.6 5.1 %collective-permute-start.10 = (bf16[40,1024]{1,0:T(8,128)(2,1)S(1)}, bf16[40,1024]{1,0:T(8,128)(2,1)S(1)}, u32[]{:S(2)}, u32[]{:S(2)}) collective-permute-start(bf16[40,1024]{1,0:T(8,128)(2,1)S(1)} %merge.1.refs_0_), channel_id=1, source_target_pairs={{0,8},{4,12},{8,0},{12,4},{16,24},{20,28},{24,16},{28,20},{1,9},{5... | collective-permute-start | bytes 245768 | tf_op jit(solution)/shard_map/ppermute | solution.py:455
  33.8 4.6 %collective-permute-start.11 = (bf16[40,1024]{1,0:T(8,128)(2,1)S(1)}, bf16[40,1024]{1,0:T(8,128)(2,1)S(1)}, u32[]{:S(2)}, u32[]{:S(2)}) collective-permute-start(bf16[40,1024]{1,0:T(8,128)(2,1)S(1)} %merge.1.refs_0_), channel_id=1, source_target_pairs={{0,16},{4,20},{8,24},{12,28},{16,0},{20,4},{24,8},{28,12},{1,17},{... | collective-permute-start | bytes 245768 | tf_op jit(solution)/shard_map/ppermute | solution.py:455
  35.1 5.3 %collective-permute-start.12 = (bf16[40,1024]{1,0:T(8,128)(2,1)S(1)}, bf16[40,1024]{1,0:T(8,128)(2,1)S(1)}, u32[]{:S(2)}, u32[]{:S(2)}) collective-permute-start(bf16[40,1024]{1,0:T(8,128)(2,1)S(1)} %merge.1.refs_0_), channel_id=1, source_target_pairs={{0,24},{4,28},{8,16},{12,20},{16,8},{20,12},{24,0},{28,4},{1,25},{... | collective-permute-start | bytes 245768 | tf_op jit(solution)/shard_map/ppermute | solution.py:455
  41.5 4.5 %collective-permute-start.14 = (bf16[40,1024]{1,0:T(8,128)(2,1)S(1)}, bf16[40,1024]{1,0:T(8,128)(2,1)S(1)}, u32[]{:S(2)}, u32[]{:S(2)}) collective-permute-start(bf16[40,1024]{1,0:T(8,128)(2,1)S(1)} %get-tuple-element.69), channel_id=1, source_target_pairs={{0,8},{4,12},{8,0},{12,4},{16,24},{20,28},{24,16},{28,20},{1,9},{5... | collective-permute-start | bytes 245768 | tf_op jit(solution)/shard_map/ppermute | solution.py:455
  42.5 4.4 %collective-permute-start.15 = (bf16[40,1024]{1,0:T(8,128)(2,1)S(1)}, bf16[40,1024]{1,0:T(8,128)(2,1)S(1)}, u32[]{:S(2)}, u32[]{:S(2)}) collective-permute-start(bf16[40,1024]{1,0:T(8,128)(2,1)S(1)} %get-tuple-element.70), channel_id=1, source_target_pairs={{0,16},{4,20},{8,24},{12,28},{16,0},{20,4},{24,8},{28,12},{1,17},{... | collective-permute-start | bytes 245768 | tf_op jit(solution)/shard_map/ppermute | solution.py:455
  43.2 5.3 %collective-permute-start.16 = (bf16[40,1024]{1,0:T(8,128)(2,1)S(1)}, bf16[40,1024]{1,0:T(8,128)(2,1)S(1)}, u32[]{:S(2)}, u32[]{:S(2)}) collective-permute-start(bf16[40,1024]{1,0:T(8,128)(2,1)S(1)} %get-tuple-element.71), channel_id=1, source_target_pairs={{0,24},{4,28},{8,16},{12,20},{16,8},{20,12},{24,0},{28,4},{1,25},{... | collective-permute-start | bytes 245768 | tf_op jit(solution)/shard_map/ppermute | solution.py:455
  48.6 6.3 %collective-permute-start.17 = (bf16[40,1024]{1,0:T(8,128)(2,1)S(1)}, bf16[40,1024]{1,0:T(8,128)(2,1)S(1)}, u32[]{:S(2)}, u32[]{:S(2)}) collective-permute-start(bf16[40,1024]{1,0:T(8,128)(2,1)S(1)} %get-tuple-element.80), channel_id=1, source_target_pairs={{0,1},{1,2},{2,3},{3,0},{4,5},{5,6},{6,7},{7,4},{8,9},{9,10},{10,1... | collective-permute-start | bytes 245768 | tf_op jit(solution)/shard_map/ppermute | solution.py:458
  50.3 5.5 %collective-permute-start.18 = (bf16[40,1024]{1,0:T(8,128)(2,1)S(1)}, bf16[40,1024]{1,0:T(8,128)(2,1)S(1)}, u32[]{:S(2)}, u32[]{:S(2)}) collective-permute-start(bf16[40,1024]{1,0:T(8,128)(2,1)S(1)} %get-tuple-element.79), channel_id=1, source_target_pairs={{0,2},{1,3},{2,0},{3,1},{4,6},{5,7},{6,4},{7,5},{8,10},{9,11},{10,... | collective-permute-start | bytes 245768 | tf_op jit(solution)/shard_map/ppermute | solution.py:458
  52.9 5.8 %collective-permute-start.19 = (bf16[40,1024]{1,0:T(8,128)(2,1)S(1)}, bf16[40,1024]{1,0:T(8,128)(2,1)S(1)}, u32[]{:S(2)}, u32[]{:S(2)}) collective-permute-start(bf16[40,1024]{1,0:T(8,128)(2,1)S(1)} %get-tuple-element.78), channel_id=1, source_target_pairs={{0,3},{1,0},{2,1},{3,2},{4,7},{5,4},{6,5},{7,6},{8,11},{9,8},{10,9... | collective-permute-start | bytes 245768 | tf_op jit(solution)/shard_map/ppermute | solution.py:458
  59.7 6.4 %collective-permute-start.20 = (bf16[40,1152]{1,0:T(8,128)(2,1)S(1)}, bf16[40,1152]{1,0:T(8,128)(2,1)S(1)}, u32[]{:S(2)}, u32[]{:S(2)}) collective-permute-start(bf16[40,1152]{1,0:T(8,128)(2,1)S(1)} %get-tuple-element.75), channel_id=1, source_target_pairs={{0,1},{1,2},{2,3},{3,0},{4,5},{5,6},{6,7},{7,4},{8,9},{9,10},{10,1... | collective-permute-start | bytes 276488 | tf_op jit(solution)/shard_map/ppermute | solution.py:458
  61.9 6.3 %collective-permute-start.21 = (bf16[40,1152]{1,0:T(8,128)(2,1)S(1)}, bf16[40,1152]{1,0:T(8,128)(2,1)S(1)}, u32[]{:S(2)}, u32[]{:S(2)}) collective-permute-start(bf16[40,1152]{1,0:T(8,128)(2,1)S(1)} %get-tuple-element.76), channel_id=1, source_target_pairs={{0,2},{1,3},{2,0},{3,1},{4,6},{5,7},{6,4},{7,5},{8,10},{9,11},{10,... | collective-permute-start | bytes 276488 | tf_op jit(solution)/shard_map/ppermute | solution.py:458
  63.5 5.5 %collective-permute-start.22 = (bf16[40,1152]{1,0:T(8,128)(2,1)S(1)}, bf16[40,1152]{1,0:T(8,128)(2,1)S(1)}, u32[]{:S(2)}, u32[]{:S(2)}) collective-permute-start(bf16[40,1152]{1,0:T(8,128)(2,1)S(1)} %get-tuple-element.77), channel_id=1, source_target_pairs={{0,3},{1,0},{2,1},{3,2},{4,7},{5,4},{6,5},{7,6},{8,11},{9,8},{10,9... | collective-permute-start | bytes 276488 | tf_op jit(solution)/shard_map/ppermute | solution.py:458
